TPU v7x, 512 devices: a whole 4x8x8 slice. The times are simulated.
512 devices in a mesh: dp: 32 (over y_lo, z), row: 4 (over x), col: 4 (over y_hi, core).
Axes of the slice: x: 4, y: 8 (y_hi: 2, y_lo: 4; y = y_hi * 4 + y_lo), z: 8, core: 2. Of those that a mesh axis runs over, the one named last changes fastest.
Arguments:
- query_out: bfloat16 [6144, 4096], P(('dp', 'row'), 'col'), may hold values from -6 to 6
- query_in: bfloat16 [6144, 4096], P(('dp', 'col')), may hold values from -6 to 6
- out_basis: bfloat16 [4096, 4096], P('col', ('dp', 'row')), may hold values from -0.09375 to 0.09375
- in_basis: bfloat16 [4096, 4096], P(('dp', 'row'), 'col'), may hold values from -0.09375 to 0.09375
- eigvals: float32 [4096, 4096], P(('dp', 'row'), 'col'), may hold values from 16 to 1024
- train_out: bfloat16 [6144, 4096], P(('dp', 'row'), 'col'), may hold values from -0.09375 to 0.09375
- train_in: bfloat16 [6144, 4096], P(('dp', 'col')), may hold values from -0.09375 to 0.09375
Outputs:
- precond: float32 [4096, 4096], P(('dp', 'row'), 'col')
- scores: float32 [6144], P('dp')
All inputs are finite; a program needn't handle non-finite values.
Results may differ from a plain program's by a relative error of at most 0.028.
Values may be sent and summed in bfloat16 or wider, within the bound.
No kernel may reach another device: no remote copies, remote signals or barrier semaphores. Data moves between devices by JAX's collectives and lax.ppermute only.
A program may use at most 64 MiB of HBM per device.

v0:
```python
import jax
import jax.numpy as jnp
from jax import lax
from jax.sharding import PartitionSpec as P

damping = 1.0


def rotate_out(tok_rows, basis_panel):
    gathered = lax.all_gather(tok_rows, "row", axis=0, tiled=True)
    partial_sum = jnp.dot(gathered, basis_panel, preferred_element_type=jnp.float32)
    return lax.psum(partial_sum.astype(jnp.bfloat16), "col")


def rotate_in(tok_rows, basis_panel):
    groups = lax.axis_size("dp")
    row_count = lax.axis_size("row")
    sub_width = tok_rows.shape[1] // (groups * row_count)
    split_rows = tok_rows.reshape(tok_rows.shape[0], groups, row_count, sub_width)
    picked = lax.dynamic_index_in_dim(split_rows, lax.axis_index("row"), 2, keepdims=False)
    picked = picked.reshape(tok_rows.shape[0], groups * sub_width)
    gathered = lax.all_gather(picked, "col", axis=0, tiled=True)
    partial_sum = jnp.dot(gathered, basis_panel, preferred_element_type=jnp.float32)
    return lax.psum(partial_sum.astype(jnp.bfloat16), "row")


def per_device(query_out, query_in, out_basis, in_basis, eigvals, train_out, train_in):
    panel_out = lax.all_gather(out_basis, "dp", axis=1, tiled=True)
    panel_in = lax.all_gather(in_basis, "dp", axis=0, tiled=True)
    query_rot = rotate_out(query_out, panel_out)
    query_inr = rotate_in(query_in, panel_in)
    partial_grad = lax.dot_general(
        query_rot, query_inr, (((0,), (0,)), ((), ())), preferred_element_type=jnp.float32
    )
    rows_own = eigvals.shape[0]
    summed = lax.psum(partial_grad.astype(jnp.bfloat16), "dp").astype(jnp.float32)
    owned = lax.dynamic_slice_in_dim(summed, lax.axis_index("dp") * rows_own, rows_own, 0)
    precond = owned / (eigvals + damping)
    shared = precond.astype(jnp.bfloat16)
    train_rot = rotate_out(train_out, panel_out)
    train_inr = rotate_in(train_in, panel_in)
    mixed = jnp.dot(
        train_rot,
        lax.all_gather(shared, "dp", axis=0, tiled=True),
        preferred_element_type=jnp.float32,
    )
    partial_scores = jnp.sum(mixed * train_inr.astype(jnp.float32), axis=1)
    scores = lax.psum(partial_scores, ("row", "col"))
    return (precond, scores)


def solution(mesh):
    in_specs = (
        P(("dp", "row"), "col"),
        P(("dp", "col"), None),
        P("col", ("dp", "row")),
        P(("dp", "row"), "col"),
        P(("dp", "row"), "col"),
        P(("dp", "row"), "col"),
        P(("dp", "col"), None),
    )
    out_specs = (P(("dp", "row"), "col"), P("dp"))
    return jax.shard_map(
        per_device, mesh=mesh, in_specs=in_specs, out_specs=out_specs, check_vma=False
    )
```

profile of v0, /device:TPU:1, one launch (start us, length us, event | category | flops | bytes accessed | tf_op | source)
XLA Modules:
  0.0 969.9 jit_solution(9535577205798143316)
XLA Ops:
  7.2 0.7 all-gather.6.cloned.1.call-update
  7.9 0.7 all-gather.4.cloned.1.call-update
  8.7 1.5 copy.9
  10.2 1.5 copy.11
  11.7 0.1 copy.14
  11.8 0.1 copy.13
  12.0 16.7 %all_gather.27 = bf16[192,1024]{1,0:T(8,128)(2,1)S(1)} all-gather(bf16[48,1024]{1,0:T(8,128)(2,1)S(1)} %copy.14), channel_id=1, replica_groups=mesh['dp'=32,'row'=4,'col'=4] {'col'}, dimensions={0}, use_global_device_ids=true | all-gather | bytes 491520 | tf_op jit(solution)/shard_map/all_gather | solution.py:22
  28.7 12.9 %all_gather.23 = bf16[192,1024]{1,0:T(8,128)(2,1)S(1)} all-gather(bf16[48,1024]{1,0:T(8,128)(2,1)S(1)} %copy.13), channel_id=1, replica_groups=mesh['dp'=32,'row'=4,'col'=4] {'col'}, dimensions={0}, use_global_device_ids=true | all-gather | bytes 491520 | tf_op jit(solution)/shard_map/all_gather | solution.py:22
  41.6 106.6 %all-gather.6.cloned.1.call-done = bf16[1024,1024]{1,0:T(8,128)(2,1)} async-done(((bf16[32,1024]{1,0:T(8,128)(2,1)}), bf16[1024,1024]{1,0:T(8,128)(2,1)}) %all-gather.6.cloned.1.call-update) | async-done | bytes 2097168 | tf_op jit(solution)/shard_map/all_gather | solution.py:29
  148.2 3.1 convolution_convert_fusion.1
  151.3 1.4 convolution_convert_fusion.3
  152.8 10.9 %all_gather.25 = bf16[192,1024]{1,0:T(8,128)(2,1)S(1)} all-gather(bf16[48,1024]{1,0:T(8,128)(2,1)S(1)} %copy-done.3), channel_id=1, replica_groups=mesh['dp'=32,'row'=4,'col'=4] {'row'}, dimensions={0}, use_global_device_ids=true | all-gather | bytes 491520 | tf_op jit(solution)/shard_map/all_gather | solution.py:10
  163.6 10.0 %all_gather.21 = bf16[192,1024]{1,0:T(8,128)(2,1)S(1)} all-gather(bf16[48,1024]{1,0:T(8,128)(2,1)S(1)} %copy-done.4), channel_id=1, replica_groups=mesh['dp'=32,'row'=4,'col'=4] {'row'}, dimensions={0}, use_global_device_ids=true | all-gather | bytes 491520 | tf_op jit(solution)/shard_map/all_gather | solution.py:10
  173.6 126.9 %all-gather.4.cloned.1.call-done = bf16[1024,1024]{0,1:T(8,128)(2,1)} async-done(((bf16[1024,32]{0,1:T(8,128)(2,1)}), bf16[1024,1024]{0,1:T(8,128)(2,1)}) %all-gather.4.cloned.1.call-update) | async-done | bytes 2097168 | tf_op jit(solution)/shard_map/all_gather | solution.py:28
  300.6 3.3 convolution_convert_fusion.2
  303.9 1.6 convolution_convert_fusion.4
  305.6 68.1 %all-reduce.10.cloned.1.call-done = (bf16[192,1024]{1,0:T(8,128)(2,1)}, bf16[192,1024]{1,0:T(8,128)(2,1)}) async-done(((bf16[192,1024]{1,0:T(8,128)(2,1)}, bf16[192,1024]{1,0:T(8,128)(2,1)}), (bf16[192,1024]{1,0:T(8,128)(2,1)}, bf16[192,1024]{1,0:T(8,128)(2,1)})) %all-reduce.10.cloned.1.call-update) | async-done | bytes 786448 | tf_op jit(solution)/shard_map/psum | solution.py:24
  373.7 75.0 %all-reduce.8.cloned.1.call-done = (bf16[192,1024]{1,0:T(8,128)(2,1)}, bf16[192,1024]{1,0:T(8,128)(2,1)}) async-done(((bf16[192,1024]{1,0:T(8,128)(2,1)}, bf16[192,1024]{1,0:T(8,128)(2,1)}), (bf16[192,1024]{1,0:T(8,128)(2,1)}, bf16[192,1024]{1,0:T(8,128)(2,1)})) %all-reduce.8.cloned.1.call-update) | async-done | bytes 786448 | tf_op jit(solution)/shard_map/psum | solution.py:12
  448.7 3.3 convolution_convert_fusion
  452.0 290.8 %all-reduce.6.cloned.1.call-done = bf16[1024,1024]{1,0:T(8,128)(2,1)} async-done(((bf16[1024,1024]{1,0:T(8,128)(2,1)}), bf16[1024,1024]{1,0:T(8,128)(2,1)}) %all-reduce.6.cloned.1.call-update) | async-done | bytes 2097168 | tf_op jit(solution)/shard_map/psum | solution.py:36
  742.8 1.5 fusion.1
  744.4 150.6 %all-gather.8.cloned.1.call-done = bf16[1024,1024]{1,0:T(8,128)(2,1)} async-done(((bf16[32,1024]{1,0:T(8,128)(2,1)}), bf16[1024,1024]{1,0:T(8,128)(2,1)}) %all-gather.8.cloned.1.call-update) | async-done | bytes 2097168 | tf_op jit(solution)/shard_map/all_gather | solution.py:44
  895.0 2.3 fusion
  897.2 65.8 %psum.47 = f32[192]{0:T(256)} all-reduce(f32[192]{0:T(256)S(1)} %fusion), channel_id=1, replica_groups=mesh['dp'=32,'row'=4,'col'=4] {'row','col'}, use_global_device_ids=true, to_apply=%region_6.7 | all-reduce | flops 192 | bytes 1536 | tf_op jit(solution)/shard_map/psum | solution.py:48
  (25 shorter events, 0.4 us)
Async XLA Ops:
  7.2 141.1 %all-gather.6.cloned.1.call-start = ((), (), s32[]{:S(2)}) async-start(), calls=%async_computation.1 | async-start | bytes 2162688 | tf_op jit(solution)/shard_map/all_gather | solution.py:29
  7.9 292.7 %all-gather.4.cloned.1.call-start = ((), (), s32[]{:S(2)}) async-start(), calls=%async_computation | async-start | bytes 2162688 | tf_op jit(solution)/shard_map/all_gather | solution.py:28
  8.6 365.1 %all-reduce.10.cloned.1.call-start = ((), (), s32[]{:S(2)}) async-start(), calls=%async_computation.5 | async-start | bytes 1572864 | tf_op jit(solution)/shard_map/psum | solution.py:24
  148.2 3.1 copy-start.1
  151.3 1.4 copy-start.3
  151.3 12.3 %copy-start.4 = (bf16[48,1024]{1,0:T(8,128)(2,1)S(1)}, bf16[48,1024]{1,0:T(8,128)(2,1)}, u32[]{:S(2)}) copy-start(bf16[48,1024]{1,0:T(8,128)(2,1)} %param.7) | copy-start | bytes 294916
  152.7 295.9 %all-reduce.8.cloned.1.call-start = ((), (), s32[]{:S(2)}) async-start(), calls=%async_computation.4 | async-start | bytes 1572864 | tf_op jit(solution)/shard_map/psum | solution.py:12
  300.6 3.3 copy-start
  305.5 437.3 %all-reduce.6.cloned.1.call-start = ((), (), s32[]{:S(2)}) async-start(), calls=%async_computation.2 | async-start | bytes 4194304 | tf_op jit(solution)/shard_map/psum | solution.py:36
  448.7 294.2 %copy-start.2 = (f32[32,1024]{1,0:T(8,128)S(1)}, f32[32,1024]{1,0:T(8,128)}, u32[]{:S(2)}) copy-start(f32[32,1024]{1,0:T(8,128)} %param.11) | copy-start | bytes 393220
  448.7 446.3 %copy-start.5 = (bf16[192,1024]{1,0:T(8,128)(2,1)S(1)}, bf16[192,1024]{1,0:T(8,128)(2,1)}, u32[]{:S(2)}) copy-start(bf16[192,1024]{1,0:T(8,128)(2,1)} %get-tuple-element.5) | copy-start | bytes 1179652
  448.7 446.3 %copy-start.6 = (bf16[192,1024]{1,0:T(8,128)(2,1)S(1)}, bf16[192,1024]{1,0:T(8,128)(2,1)}, u32[]{:S(2)}) copy-start(bf16[192,1024]{1,0:T(8,128)(2,1)} %get-tuple-element.3) | copy-start | bytes 1179652
  452.0 443.0 %all-gather.8.cloned.1.call-start = ((), (), s32[]{:S(2)}) async-start(), calls=%async_computation.3 | async-start | bytes 2162688 | tf_op jit(solution)/shard_map/all_gather | solution.py:44
Sparse Core Ops, SparseCore 0:
  10.0 138.1 all-gather.5
  150.3 150.2 all-gather.3
  303.0 70.6 all-reduce.9
  376.6 72.0 all-reduce.7
  452.1 290.6 all-reduce.5
  744.7 150.1 all-gather.7
where the time goes:
time: 970 us
  waiting for transfers between devices  819 us (84%)
  blocking collectives  116 us (12%)
  matrix products  14.9 us (2%)
  between operations  14.2 us (1%)
    psum x1, waiting for transfers between devices, per_device(): lax.psum(partial_grad.astype(jnp.bfloat16), 'dp').astype(jnp.float32)  291 us
    all_gather x1, waiting for transfers between devices, per_device(): lax.all_gather(shared, 'dp', axis=0, tiled=True)  151 us
    all_gather x1, waiting for transfers between devices, per_device(): panel_out = lax.all_gather(out_basis, 'dp', axis=1, tiled=True)  127 us
    all_gather x1, waiting for transfers between devices, per_device(): panel_in = lax.all_gather(in_basis, 'dp', axis=0, tiled=True)  107 us
    psum x1, waiting for transfers between devices, rotate_out(): return lax.psum(partial_sum.astype(jnp.bfloat16), 'col')  75 us
    psum x1, waiting for transfers between devices, rotate_in(): return lax.psum(partial_sum.astype(jnp.bfloat16), 'row')  68.1 us
    psum x1, blocking collectives, per_device(): scores = lax.psum(partial_scores, ('row', 'col'))  65.8 us
    all_gather x2, blocking collectives, rotate_in(): gathered = lax.all_gather(picked, 'col', axis=0, tiled=True)  29.6 us
  transfers between devices with their start and end apart: 6, of which 6 were waited for; matrix products, arithmetic and copies ran while one was open for 1% of the time, Pallas kernels for 0%

commit v1 on v0

v1 whole, which is shorter than its diff:
```python
import jax
import jax.numpy as jnp
from jax import lax
from jax.sharding import Mesh, PartitionSpec as P

damping = 1.0
f32, bf16 = jnp.float32, jnp.bfloat16
DP = ("y", "z")
COL = ("h", "c")


def exchange(blocks, axes):
    return lax.all_to_all(blocks, axes, 0, 0, tiled=True)


def gather(block, axes):
    count = lax.axis_size(axes)
    return exchange(jnp.broadcast_to(block[None], (count,) + block.shape), axes)


def total(blocks):
    return jnp.sum(blocks.astype(f32), axis=0)


def all_sum(partial, axes):
    count = lax.axis_size(axes)
    two, tokens, width = partial.shape
    parts = partial.astype(bf16).reshape(two, count, tokens // count, width)
    mine = total(exchange(parts.transpose(1, 0, 2, 3), axes)).astype(bf16)
    return gather(mine, axes).transpose(1, 0, 2, 3).reshape(two, tokens, width)


def gather_tokens(block, axes):
    two, rows, width = block.shape
    return gather(block, axes).transpose(1, 0, 2, 3).reshape(two, -1, width)


def dot(left, right, dims):
    return lax.dot_general(left, right, (dims, ((), ())), preferred_element_type=f32)


def per_device(query_out, query_in, out_basis, in_basis, eigvals, train_out, train_in):
    groups = lax.axis_size(DP)
    row_count = lax.axis_size("x")
    rows_own = eigvals.shape[0]

    both = gather(jnp.concatenate([out_basis.T, in_basis], axis=0), DP)
    panel_out = both[:, :rows_own].reshape(groups * rows_own, -1)
    panel_in = both[:, rows_own:].reshape(groups * rows_own, -1)

    tok_out = gather_tokens(jnp.stack([query_out, train_out]), "x")
    split = jnp.stack([query_in, train_in])
    rows = split.shape[1]
    split = split.reshape(2, rows, groups, row_count, -1)
    picked = lax.dynamic_index_in_dim(split, lax.axis_index("x"), 3, keepdims=False)
    tok_in = gather_tokens(picked.reshape(2, rows, -1), COL)

    rot = all_sum(dot(tok_out, panel_out, ((2,), (1,))), COL)
    inr = all_sum(dot(tok_in, panel_in, ((2,), (0,))), "x")

    partial_grad = dot(rot[0], inr[0], ((0,), (0,))).astype(bf16)
    grad = total(exchange(partial_grad.reshape(groups, rows_own, -1), DP))
    precond = grad / (eigvals + damping)
    shared = gather(precond.astype(bf16), DP).reshape(groups * rows_own, -1)
    mixed = dot(rot[1], shared, ((1,), (0,)))
    partial_scores = jnp.sum(mixed * inr[1].astype(f32), axis=1)
    scores = lax.psum(lax.psum(partial_scores, COL), "x")
    return precond, scores


def solution(mesh):
    groups, row_count, cols = mesh.devices.shape
    sizes = (4, groups // 4, row_count, 2, cols // 2)
    fine = Mesh(mesh.devices.reshape(sizes), ("y", "z", "x", "h", "c"))
    in_specs = (
        P(("y", "z", "x"), COL),
        P(("y", "z", "h", "c"), None),
        P(COL, ("y", "z", "x")),
        P(("y", "z", "x"), COL),
        P(("y", "z", "x"), COL),
        P(("y", "z", "x"), COL),
        P(("y", "z", "h", "c"), None),
    )
    out_specs = (P(("y", "z", "x"), COL), P(DP))
    return jax.shard_map(
        per_device, mesh=fine, in_specs=in_specs, out_specs=out_specs, check_vma=False
    )
```

time: 970 us -> 431 us (0.44)
  waiting for transfers between devices: 819 us -> 233 us
  starting transfers between devices: 0.24 us -> 77.6 us
  blocking collectives: 116 us -> 87.9 us
  local copies, waits for them, and re-layouts: 3.26 us -> 19.2 us
  between operations: 14.2 us -> 0.83 us
  matrix products: 14.9 us -> 5.02 us
    psum x3 -> x0, waiting for transfers between devices: 434 us -> none  [the longest x1 291 us: per_device(): lax.psum(partial_grad.astype(jnp.bfloat16), 'dp').astype(jnp.float32)]
    all_gather x3 -> x0, waiting for transfers between devices: 384 us -> none  [the longest x1 151 us: per_device(): lax.all_gather(shared, 'dp', axis=0, tiled=True)]
    all_to_all x0 -> x8, waiting for transfers between devices: none -> 233 us  [exchange(): return lax.all_to_all(blocks, axes, 0, 0, tiled=True)]
    all_to_all x0 -> x8, starting transfers between devices: none -> 77.6 us  [exchange(): return lax.all_to_all(blocks, axes, 0, 0, tiled=True)]
    all_to_all x0 -> x1, blocking collectives: none -> 66.8 us  [exchange(): return lax.all_to_all(blocks, axes, 0, 0, tiled=True)]
    all_gather x4 -> x0, blocking collectives: 50.5 us -> none  [the longest x2 29.6 us: rotate_in(): gathered = lax.all_gather(picked, 'col', axis=0, tiled=True)]
    psum x1 -> x2, blocking collectives: 65.8 us -> 21.1 us  [per_device(): scores = lax.psum(lax.psum(partial_scores, COL), 'x')]
    dot_general x6 -> x4, matrix products: 14.9 us -> 5.02 us  [dot(): lax.dot_general(left, right, (dims, ((), ())), preferred_element_type=f32)]
  transfers between devices with their start and end apart: 6 -> 8, of which waited for: 6 -> 8; matrix products, arithmetic and copies ran while one was open for 1% -> 3% of each run, Pallas kernels for 0% -> 0%
where the time goes in v1:
time: 431 us; the launch traced here: 425 us
  waiting for transfers between devices  233 us (54%)
  blocking collectives  87.9 us (20%)
  starting transfers between devices  77.6 us (18%)
  local copies, waits for them, and re-layouts  19.2 us (4%)
  matrix products  5.02 us (1%)
    all_to_all x8, waiting for transfers between devices, exchange(): return lax.all_to_all(blocks, axes, 0, 0, tiled=True)  233 us
    all_to_all x8, starting transfers between devices, exchange(): return lax.all_to_all(blocks, axes, 0, 0, tiled=True)  77.6 us
    all_to_all x1, blocking collectives, exchange(): return lax.all_to_all(blocks, axes, 0, 0, tiled=True)  66.8 us
    psum x2, blocking collectives, per_device(): scores = lax.psum(lax.psum(partial_scores, COL), 'x')  21.1 us
  transfers between devices with their start and end apart: 8, of which 8 were waited for; matrix products, arithmetic and copies ran while one was open for 3% of the time, Pallas kernels for 0%

profile of v1, /device:TPU:1, one launch (start us, length us, event | category | flops | bytes accessed | tf_op | source)
XLA Modules:
  0.0 425.1 jit_solution(13287156355427654859)
XLA Ops:
  2.1 1.5 copy.16
  4.9 10.3 %all-to-all-start.4 = ((bf16[4,2,48,1024]{3,2,1,0:T(8,128)(2,1)}), bf16[4,2,48,1024]{3,2,1,0:T(8,128)(2,1)S(1)}, u32[]{:S(2)}, u32[]{:S(2)}) async-start(bf16[4,2,48,1024]{3,2,1,0:T(8,128)(2,1)} %broadcast_in_dim.18), calls=%async_computation.4 | async-start | bytes 1572864 | tf_op jit(solution)/shard_map/all_to_all | solution.py:13
  15.3 19.6 %all-to-all-done.4 = bf16[4,2,48,1024]{3,2,1,0:T(8,128)(2,1)S(1)} async-done(((bf16[4,2,48,1024]{3,2,1,0:T(8,128)(2,1)}), bf16[4,2,48,1024]{3,2,1,0:T(8,128)(2,1)S(1)}, u32[]{:S(2)}, u32[]{:S(2)}) %all-to-all-start.4) | async-done | bytes 786464 | tf_op jit(solution)/shard_map/all_to_all | solution.py:13
  34.9 2.5 broadcast_in_dim.15
  37.4 12.7 %all-to-all-start.1 = ((bf16[32,64,1024]{2,1,0:T(8,128)(2,1)}), bf16[32,64,1024]{2,1,0:T(8,128)(2,1)}, u32[]{:S(2)}, u32[]{:S(2)}) async-start(bf16[32,64,1024]{2,1,0:T(8,128)(2,1)} %broadcast_in_dim.15), calls=%async_computation.1 | async-start | bytes 8388608 | tf_op jit(solution)/shard_map/all_to_all | solution.py:13
  50.2 103.5 %all-to-all-done.1 = bf16[32,64,1024]{2,1,0:T(8,128)(2,1)} async-done(((bf16[32,64,1024]{2,1,0:T(8,128)(2,1)}), bf16[32,64,1024]{2,1,0:T(8,128)(2,1)}, u32[]{:S(2)}, u32[]{:S(2)}) %all-to-all-start.1) | async-done | bytes 4194336 | tf_op jit(solution)/shard_map/all_to_all | solution.py:13
  154.7 4.0 all-to-all-start
  158.7 4.1 fusion.3
  164.8 3.3 all-to-all-done
  168.1 3.5 all-to-all-start.5
  171.7 2.6 convolution_convert_fusion.1
  175.2 4.7 %all-to-all-done.5 = bf16[4,2,48,1024]{3,2,1,0:T(8,128)(2,1)S(1)} async-done(((bf16[4,2,48,1024]{3,2,1,0:T(8,128)(2,1)}), bf16[4,2,48,1024]{3,2,1,0:T(8,128)(2,1)S(1)}, u32[]{:S(2)}, u32[]{:S(2)}) %all-to-all-start.5) | async-done | bytes 786464 | tf_op jit(solution)/shard_map/all_to_all | solution.py:13
  179.9 27.9 %all-to-all-start.2 = ((bf16[4,2,48,1024]{3,2,1,0:T(8,128)(2,1)}), bf16[4,2,48,1024]{3,2,1,0:T(8,128)(2,1)S(1)}, u32[]{:S(2)}, u32[]{:S(2)}) async-start(bf16[4,2,48,1024]{3,2,1,0:T(8,128)(2,1)} %bitcast.48), calls=%async_computation.2 | async-start | bytes 1572864 | tf_op jit(solution)/shard_map/all_to_all | solution.py:13
  208.0 20.0 %all-to-all-done.2 = bf16[4,2,48,1024]{3,2,1,0:T(8,128)(2,1)S(1)} async-done(((bf16[4,2,48,1024]{3,2,1,0:T(8,128)(2,1)}), bf16[4,2,48,1024]{3,2,1,0:T(8,128)(2,1)S(1)}, u32[]{:S(2)}, u32[]{:S(2)}) %all-to-all-start.2) | async-done | bytes 786464 | tf_op jit(solution)/shard_map/all_to_all | solution.py:13
  229.0 3.5 all-to-all-start.6
  232.6 11.1 %all-to-all-done.6 = bf16[4,2,48,1024]{3,2,1,0:T(8,128)(2,1)S(1)} async-done(((bf16[4,2,48,1024]{3,2,1,0:T(8,128)(2,1)}), bf16[4,2,48,1024]{3,2,1,0:T(8,128)(2,1)S(1)}, u32[]{:S(2)}, u32[]{:S(2)}) %all-to-all-start.6) | async-done | bytes 786464 | tf_op jit(solution)/shard_map/all_to_all | solution.py:13
  244.7 6.9 %all-to-all-start.3 = ((bf16[4,2,48,1024]{3,2,1,0:T(8,128)(2,1)}), bf16[4,2,48,1024]{3,2,1,0:T(8,128)(2,1)S(1)}, u32[]{:S(2)}, u32[]{:S(2)}) async-start(bf16[4,2,48,1024]{3,2,1,0:T(8,128)(2,1)} %broadcast_in_dim.16), calls=%async_computation.3 | async-start | bytes 1572864 | tf_op jit(solution)/shard_map/all_to_all | solution.py:13
  251.7 18.0 %all-to-all-done.3 = bf16[4,2,48,1024]{3,2,1,0:T(8,128)(2,1)S(1)} async-done(((bf16[4,2,48,1024]{3,2,1,0:T(8,128)(2,1)}), bf16[4,2,48,1024]{3,2,1,0:T(8,128)(2,1)S(1)}, u32[]{:S(2)}, u32[]{:S(2)}) %all-to-all-start.3) | async-done | bytes 786464 | tf_op jit(solution)/shard_map/all_to_all | solution.py:13
  270.6 66.8 %all_to_all.45 = bf16[32,32,1024]{2,1,0:T(8,128)(2,1)S(1)} all-to-all(bf16[32,32,1024]{2,1,0:T(8,128)(2,1)S(1)} %bitcast.54), channel_id=1, replica_groups=mesh['y'=4,'z'=8,'x'=4,'h'=2,'c'=2] {'y','z'}, dimensions={0} | all-to-all | bytes 4194304 | tf_op jit(solution)/shard_map/all_to_all | solution.py:13
  339.0 1.6 broadcast_in_dim.20
  340.6 8.8 %all-to-all-start.8 = ((bf16[32,32,1024]{2,1,0:T(8,128)(2,1)}), bf16[32,32,1024]{2,1,0:T(8,128)(2,1)S(1)}, u32[]{:S(2)}, u32[]{:S(2)}) async-start(bf16[32,32,1024]{2,1,0:T(8,128)(2,1)} %broadcast_in_dim.20), calls=%async_computation.8 | async-start | bytes 4194304 | tf_op jit(solution)/shard_map/all_to_all | solution.py:13
  350.5 52.7 %all-to-all-done.8 = bf16[32,32,1024]{2,1,0:T(8,128)(2,1)S(1)} async-done(((bf16[32,32,1024]{2,1,0:T(8,128)(2,1)}), bf16[32,32,1024]{2,1,0:T(8,128)(2,1)S(1)}, u32[]{:S(2)}, u32[]{:S(2)}) %all-to-all-start.8) | async-done | bytes 2097184 | tf_op jit(solution)/shard_map/all_to_all | solution.py:13
  403.9 13.7 %psum.14 = f32[192]{0:T(256)S(1)} all-reduce(f32[192]{0:T(256)S(1)} %fusion), channel_id=1, replica_groups=mesh['y'=4,'z'=8,'x'=4,'h'=2,'c'=2] {'h','c'}, use_global_device_ids=true, to_apply=%region_4.5 | all-reduce | flops 192 | bytes 1536 | tf_op jit(solution)/shard_map/psum | solution.py:67
  417.7 7.4 %psum.15 = f32[192]{0:T(256)} all-reduce(f32[192]{0:T(256)S(1)} %psum.14), channel_id=1, replica_groups=mesh['y'=4,'z'=8,'x'=4,'h'=2,'c'=2] {'x'}, use_global_device_ids=true, to_apply=%region_5.6 | all-reduce | flops 192 | bytes 1536 | tf_op jit(solution)/shard_map/psum | solution.py:67
  (36 shorter events, 13.4 us)
Async XLA Ops:
  3.7 11.5 %copy-start.4 = (bf16[32,1024]{1,0:T(8,128)(2,1)S(1)}, bf16[32,1024]{1,0:T(8,128)(2,1)}, u32[]{:S(2)}) copy-start(bf16[32,1024]{1,0:T(8,128)(2,1)} %param.10) | copy-start | bytes 196612
  3.7 11.5 %copy-start.5 = (bf16[1024,32]{0,1:T(8,128)(2,1)S(1)}, bf16[1024,32]{0,1:T(8,128)(2,1)}, u32[]{:S(2)}) copy-start(bf16[1024,32]{0,1:T(8,128)(2,1)} %param.9) | copy-start | bytes 196612
  4.9 30.0 %all-to-all-start.4 = ((bf16[4,2,48,1024]{3,2,1,0:T(8,128)(2,1)}), bf16[4,2,48,1024]{3,2,1,0:T(8,128)(2,1)S(1)}, u32[]{:S(2)}, u32[]{:S(2)}) async-start(bf16[4,2,48,1024]{3,2,1,0:T(8,128)(2,1)} %broadcast_in_dim.18), calls=%async_computation.4 | async-start | bytes 1572864 | tf_op jit(solution)/shard_map/all_to_all | solution.py:13
  37.4 12.7 %copy-start.2 = (bf16[48,1024]{1,0:T(8,128)(2,1)S(1)}, bf16[48,1024]{1,0:T(8,128)(2,1)}, u32[]{:S(2)}) copy-start(bf16[48,1024]{1,0:T(8,128)(2,1)} %param.12) | copy-start | bytes 294916
  37.4 12.7 %copy-start.3 = (bf16[48,1024]{1,0:T(8,128)(2,1)S(1)}, bf16[48,1024]{1,0:T(8,128)(2,1)}, u32[]{:S(2)}) copy-start(bf16[48,1024]{1,0:T(8,128)(2,1)} %param.7) | copy-start | bytes 294916
  37.4 116.3 %all-to-all-start.1 = ((bf16[32,64,1024]{2,1,0:T(8,128)(2,1)}), bf16[32,64,1024]{2,1,0:T(8,128)(2,1)}, u32[]{:S(2)}, u32[]{:S(2)}) async-start(bf16[32,64,1024]{2,1,0:T(8,128)(2,1)} %broadcast_in_dim.15), calls=%async_computation.1 | async-start | bytes 8388608 | tf_op jit(solution)/shard_map/all_to_all | solution.py:13
  154.7 13.4 %all-to-all-start = ((bf16[4,2,48,1024]{3,2,1,0:T(8,128)(2,1)}), bf16[4,2,48,1024]{3,2,1,0:T(8,128)(2,1)S(1)}, u32[]{:S(2)}, u32[]{:S(2)}) async-start(bf16[4,2,48,1024]{3,2,1,0:T(8,128)(2,1)} %broadcast_in_dim.14), calls=%async_computation | async-start | bytes 1572864 | tf_op jit(solution)/shard_map/all_to_all | solution.py:13
  168.1 11.8 %all-to-all-start.5 = ((bf16[4,2,48,1024]{3,2,1,0:T(8,128)(2,1)}), bf16[4,2,48,1024]{3,2,1,0:T(8,128)(2,1)S(1)}, u32[]{:S(2)}, u32[]{:S(2)}) async-start(bf16[4,2,48,1024]{3,2,1,0:T(8,128)(2,1)} %bitcast.46), calls=%async_computation.5 | async-start | bytes 1572864 | tf_op jit(solution)/shard_map/all_to_all | solution.py:13
  179.9 48.1 %all-to-all-start.2 = ((bf16[4,2,48,1024]{3,2,1,0:T(8,128)(2,1)}), bf16[4,2,48,1024]{3,2,1,0:T(8,128)(2,1)S(1)}, u32[]{:S(2)}, u32[]{:S(2)}) async-start(bf16[4,2,48,1024]{3,2,1,0:T(8,128)(2,1)} %bitcast.48), calls=%async_computation.2 | async-start | bytes 1572864 | tf_op jit(solution)/shard_map/all_to_all | solution.py:13
  229.0 14.7 %all-to-all-start.6 = ((bf16[4,2,48,1024]{3,2,1,0:T(8,128)(2,1)}), bf16[4,2,48,1024]{3,2,1,0:T(8,128)(2,1)S(1)}, u32[]{:S(2)}, u32[]{:S(2)}) async-start(bf16[4,2,48,1024]{3,2,1,0:T(8,128)(2,1)} %broadcast_in_dim.19), calls=%async_computation.6 | async-start | bytes 1572864 | tf_op jit(solution)/shard_map/all_to_all | solution.py:13
  244.7 25.0 %all-to-all-start.3 = ((bf16[4,2,48,1024]{3,2,1,0:T(8,128)(2,1)}), bf16[4,2,48,1024]{3,2,1,0:T(8,128)(2,1)S(1)}, u32[]{:S(2)}, u32[]{:S(2)}) async-start(bf16[4,2,48,1024]{3,2,1,0:T(8,128)(2,1)} %broadcast_in_dim.16), calls=%async_computation.3 | async-start | bytes 1572864 | tf_op jit(solution)/shard_map/all_to_all | solution.py:13
  269.7 0.9 copy-start
  337.4 0.9 copy-start.1
  340.6 62.6 %all-to-all-start.8 = ((bf16[32,32,1024]{2,1,0:T(8,128)(2,1)}), bf16[32,32,1024]{2,1,0:T(8,128)(2,1)S(1)}, u32[]{:S(2)}, u32[]{:S(2)}) async-start(bf16[32,32,1024]{2,1,0:T(8,128)(2,1)} %broadcast_in_dim.20), calls=%async_computation.8 | async-start | bytes 4194304 | tf_op jit(solution)/shard_map/all_to_all | solution.py:13

commit v2 on v1

v2 whole, which is shorter than its diff:
```python
import jax
import jax.numpy as jnp
from jax import lax
from jax.sharding import Mesh, PartitionSpec as P

damping = 1.0
f32, bf16 = jnp.float32, jnp.bfloat16
PEERS = ("y", "z1")
COL = ("h", "c")


def exchange(blocks, axes):
    return lax.all_to_all(blocks, axes, 0, 0, tiled=True)


def gather(block, axes):
    count = lax.axis_size(axes)
    return exchange(jnp.broadcast_to(block[None], (count,) + block.shape), axes)


def shift(block, step):
    count = lax.axis_size(("z1", "z0"))
    return lax.ppermute(block, ("z1", "z0"), [(i, (i + step) % count) for i in range(count)])


def swap(block, axis):
    return lax.ppermute(block, axis, [(0, 1), (1, 0)])


def total(blocks):
    return jnp.sum(blocks.astype(f32), axis=0)


def split_tokens(partial, count):
    two, tokens, width = partial.shape
    return partial.reshape(two, count, tokens // count, width).transpose(1, 0, 2, 3)


def join_tokens(parts):
    count, two, rows, width = parts.shape
    return parts.transpose(1, 0, 2, 3).reshape(two, count * rows, width)


def dot(left, right, dims):
    return lax.dot_general(left, right, (dims, ((), ())), preferred_element_type=f32)


def per_device(query_out, query_in, out_basis, in_basis, eigvals, train_out, train_in):
    peers = lax.axis_size(PEERS)
    row_count = lax.axis_size("x")
    rows_own, width = eigvals.shape
    parity, side = lax.axis_index("z0"), lax.axis_index("h")
    flat = (peers * rows_own, width)

    split = jnp.stack([query_in, train_in])
    rows = split.shape[1]
    split = split.reshape(2, rows, peers, 2 * row_count, -1)

    def pick(which):
        index = which * row_count + lax.axis_index("x")
        part = lax.dynamic_index_in_dim(split, index, 3, keepdims=False)
        return part.reshape(2, rows, -1)

    picked = jnp.concatenate([pick(parity), pick(1 - parity)], axis=2)
    far = swap(picked, "h")
    pair = jnp.where(side == 0, jnp.stack([picked, far]), jnp.stack([far, picked]))
    near = gather(pair, "c")
    tok_in = join_tokens(near.transpose(1, 0, 2, 3, 4).reshape((-1,) + near.shape[2:]))
    tok_out = join_tokens(gather(jnp.stack([query_out, train_out]), "x"))

    panel_in = gather(in_basis, PEERS).reshape(flat)
    panel_out = gather(out_basis.T, PEERS).reshape(flat[0], -1)
    panel_in_other = shift(panel_in, 1)
    panel_out_other = shift(panel_out, -1)

    half = flat[0]
    inr = dot(tok_in[..., :half], panel_in, ((2,), (0,)))
    inr = inr + dot(tok_in[..., half:], panel_in_other, ((2,), (0,)))
    inr = total(exchange(split_tokens(inr.astype(bf16), row_count), "x")).astype(bf16)
    inr = join_tokens(gather(inr, "x"))

    panels = jnp.concatenate([panel_out, panel_out_other], axis=0)
    rot = dot(tok_out, panels, ((2,), (1,))).astype(bf16)
    rot = total(exchange(split_tokens(rot, 2), "c")).astype(bf16)
    rot = (rot.astype(f32) + swap(rot, "h").astype(f32)).astype(bf16)
    rot = join_tokens(gather(rot, "c"))

    partial_grad = dot(rot[0], inr[0], ((0,), (0,))).astype(bf16)
    own, other = partial_grad[:half], partial_grad[half:]
    cut = half // 2
    low, high = shift(other[:cut], 1), shift(other[cut:], -1)
    own = own.astype(f32) + jnp.concatenate([low, high], axis=0).astype(f32)
    grad = total(exchange(own.astype(bf16).reshape(peers, rows_own, width), PEERS))
    precond = grad / (eigvals + damping)

    shared = gather(precond.astype(bf16), PEERS).reshape(flat)
    low, high = shift(shared[:cut], 1), shift(shared[cut:], -1)
    mixed = dot(rot[1], jnp.concatenate([shared, low, high], axis=0), ((1,), (0,)))
    partial_scores = jnp.sum(mixed * inr[1].astype(f32), axis=1)
    scores = total(gather(partial_scores, ("x",) + COL))
    return precond, scores


def solution(mesh):
    groups, row_count, cols = mesh.devices.shape
    sizes = (4, groups // 8, 2, row_count, 2, cols // 2)
    fine = Mesh(mesh.devices.reshape(sizes), ("y", "z1", "z0", "x", "h", "c"))
    dp = ("y", "z1", "z0")
    by_rows, by_tokens = P(dp + ("x",), COL), P(dp + COL, None)
    in_specs = (
        by_rows,
        by_tokens,
        P(COL, dp + ("x",)),
        by_rows,
        by_rows,
        by_rows,
        by_tokens,
    )
    return jax.shard_map(
        per_device, mesh=fine, in_specs=in_specs, out_specs=(by_rows, P(dp)), check_vma=False
    )
```

time: 431 us -> 312 us (0.72)
  waiting for transfers between devices: 233 us -> 84.3 us
  blocking collectives: 87.9 us -> 132 us
  starting transfers between devices: 77.6 us -> 61.8 us
    all_to_all x8 -> x5, waiting for transfers between devices: 233 us -> 45 us  [exchange(): return lax.all_to_all(blocks, axes, 0, 0, tiled=True)]
    all_to_all x1 -> x6, blocking collectives: 66.8 us -> 132 us  [exchange(): return lax.all_to_all(blocks, axes, 0, 0, tiled=True)]
    all_to_all x8 -> x5, starting transfers between devices: 77.6 us -> 23.4 us  [exchange(): return lax.all_to_all(blocks, axes, 0, 0, tiled=True)]
    ppermute x0 -> x8, waiting for transfers between devices: none -> 39.3 us  [the longest x6 28.2 us: shift(): lax.ppermute(block, ('z1', 'z0'), [(i, (i + step) % count) for i in range...]
    ppermute x0 -> x8, starting transfers between devices: none -> 38.4 us  [the longest x6 23.8 us: shift(): lax.ppermute(block, ('z1', 'z0'), [(i, (i + step) % count) for i in range...]
    psum x2 -> x0, blocking collectives: 21.1 us -> none  [per_device(): scores = lax.psum(lax.psum(partial_scores, COL), 'x')]
    dynamic_slice x0 -> x1, local copies, waits for them, and re-layouts: none -> 7.89 us  [pick(): part = lax.dynamic_index_in_dim(split, index, 3, keepdims=False)]
    slice x2 -> x3, local copies, waits for them, and re-layouts: 5.17 us -> 0.21 us  [the longest x1 0.09 us: per_device(): low, high = (shift(shared[:cut], 1), shift(shared[cut:], -1))]
  transfers between devices with their start and end apart: 8 -> 13, of which waited for: 8 -> 12; matrix products, arithmetic and copies ran while one was open for 3% -> 3% of each run, Pallas kernels for 0% -> 0%
where the time goes in v2:
time: 312 us; the launch traced here: 310 us
  blocking collectives  132 us (42%)
  waiting for transfers between devices  84.3 us (27%)
  starting transfers between devices  61.8 us (20%)
  local copies, waits for them, and re-layouts  20.5 us (7%)
  matrix products  6.48 us (2%)
  other arithmetic  3.24 us (1%)
    all_to_all x6, blocking collectives, exchange(): return lax.all_to_all(blocks, axes, 0, 0, tiled=True)  132 us
    all_to_all x5, waiting for transfers between devices, exchange(): return lax.all_to_all(blocks, axes, 0, 0, tiled=True)  45 us
    ppermute x6, waiting for transfers between devices, shift(): lax.ppermute(block, ('z1', 'z0'), [(i, (i + step) % count) for i in range...  28.2 us
    ppermute x6, starting transfers between devices, shift(): lax.ppermute(block, ('z1', 'z0'), [(i, (i + step) % count) for i in range...  23.8 us
    all_to_all x5, starting transfers between devices, exchange(): return lax.all_to_all(blocks, axes, 0, 0, tiled=True)  23.4 us
    ppermute x2, starting transfers between devices, swap(): return lax.ppermute(block, axis, [(0, 1), (1, 0)])  14.6 us
    ppermute x2, waiting for transfers between devices, swap(): return lax.ppermute(block, axis, [(0, 1), (1, 0)])  11.1 us
    dynamic_slice x1, local copies, waits for them, and re-layouts, pick(): part = lax.dynamic_index_in_dim(split, index, 3, keepdims=False)  7.89 us
  transfers between devices with their start and end apart: 13, of which 12 were waited for; matrix products, arithmetic and copies ran while one was open for 3% of the time, Pallas kernels for 0%

profile of v2, /device:TPU:1, one launch (start us, length us, event | category | flops | bytes accessed | tf_op | source)
XLA Modules:
  0.0 309.6 jit_solution(15150202293750563650)
XLA Ops:
  6.7 7.9 %dynamic-slice_reduce_fusion = (bf16[2,48,16,32]{3,2,1,0:T(8,128)(2,1)S(1)}, bf16[2,48,16,32]{3,2,1,0:T(8,128)(2,1)S(1)}) fusion(bf16[2,48,16,8,32]{4,3,2,1,0:T(8,128)(2,1)} %constant_dynamic-update-slice_fusion, s32[]{:T(128)S(6)} %select_n.21, s32[]{:T(128)S(6)} %select_n.20), kind=kLoop, calls=%fused_computation.20 | loop fusion | bytes 393224 | tf_op jit(solution)/shard_map/jit(dynamic_index_in_dim)/dynamic_slice | solution.py:61
  15.3 8.3 %collective-permute-start.2 = (bf16[2,48,1024]{2,1,0:T(8,128)(2,1)S(1)}, bf16[2,48,1024]{2,1,0:T(8,128)(2,1)S(1)}, u32[]{:S(2)}, u32[]{:S(2)}) collective-permute-start(bf16[2,48,1024]{2,1,0:T(8,128)(2,1)S(1)} %constant_dynamic-update-slice_fusion.2), channel_id=1, source_target_pairs={{0,2},{2,0},{1,3},{3,1},{4,6},{6,4},{5,7},{7,5},{8,10},{10,8},{9,1... | collective-permute-start | bytes 589832 | tf_op jit(solution)/shard_map/ppermute | solution.py:27
  23.6 7.8 %collective-permute-done.2 = bf16[2,48,1024]{2,1,0:T(8,128)(2,1)S(1)} collective-permute-done((bf16[2,48,1024]{2,1,0:T(8,128)(2,1)S(1)}, bf16[2,48,1024]{2,1,0:T(8,128)(2,1)S(1)}, u32[]{:S(2)}, u32[]{:S(2)}) %collective-permute-start.2) | collective-permute-done | bytes 196640 | tf_op jit(solution)/shard_map/ppermute | solution.py:27
  31.6 8.9 %all_to_all.56 = bf16[2,2,2,48,1024]{4,3,1,2,0:T(8,128)(2,1)S(1)} all-to-all(bf16[2,2,2,48,1024]{4,3,1,2,0:T(8,128)(2,1)S(1)} %broadcast_in_dim.19), channel_id=1, replica_groups=mesh['y'=4,'z1'=4,'z0'=2,'x'=4,'h'=2,'c'=2] {'c'}, dimensions={0} | all-to-all | bytes 1572864 | tf_op jit(solution)/shard_map/all_to_all | solution.py:13
  40.6 35.6 %all_to_all.57 = bf16[16,32,1024]{2,1,0:T(8,128)(2,1)} all-to-all(bf16[16,32,1024]{2,1,0:T(8,128)(2,1)S(1)} %broadcast_in_dim.17), channel_id=1, replica_groups=mesh['y'=4,'z1'=4,'z0'=2,'x'=4,'h'=2,'c'=2] {'y','z1'}, dimensions={0} | all-to-all | bytes 2097152 | tf_op jit(solution)/shard_map/all_to_all | solution.py:13
  77.3 6.6 %all-to-all-start.5 = ((bf16[16,32,1024]{2,1,0:T(8,128)(2,1)}), bf16[16,32,1024]{2,1,0:T(8,128)(2,1)S(1)}, u32[]{:S(2)}, u32[]{:S(2)}) async-start(bf16[16,32,1024]{2,1,0:T(8,128)(2,1)} %broadcast_in_dim.20), calls=%async_computation.5 | async-start | bytes 2097152 | tf_op jit(solution)/shard_map/all_to_all | solution.py:13
  83.9 5.3 %collective-permute-start = (bf16[512,1024]{1,0:T(8,128)(2,1)}, bf16[512,1024]{1,0:T(8,128)(2,1)}, u32[]{:S(2)}, u32[]{:S(2)}) collective-permute-start(bf16[512,1024]{1,0:T(8,128)(2,1)} %bitcast.5), channel_id=1, source_target_pairs={{0,112},{16,0},{32,16},{48,32},{64,48},{80,64},{96,80},{112,96},{1... | collective-permute-start | bytes 3145736 | tf_op jit(solution)/shard_map/ppermute | solution.py:23
  89.2 18.8 %all-to-all-done.5 = bf16[16,32,1024]{2,1,0:T(8,128)(2,1)S(1)} async-done(((bf16[16,32,1024]{2,1,0:T(8,128)(2,1)}), bf16[16,32,1024]{2,1,0:T(8,128)(2,1)S(1)}, u32[]{:S(2)}, u32[]{:S(2)}) %all-to-all-start.5) | async-done | bytes 1048608 | tf_op jit(solution)/shard_map/all_to_all | solution.py:13
  109.0 4.0 %all-to-all-start = ((bf16[4,2,48,1024]{3,2,1,0:T(8,128)(2,1)}), bf16[4,2,48,1024]{3,2,1,0:T(8,128)(2,1)S(1)}, u32[]{:S(2)}, u32[]{:S(2)}) async-start(bf16[4,2,48,1024]{3,2,1,0:T(8,128)(2,1)} %broadcast_in_dim.16), calls=%async_computation | async-start | bytes 1572864 | tf_op jit(solution)/shard_map/all_to_all | solution.py:13
  116.5 4.8 %all-to-all-done = bf16[4,2,48,1024]{3,2,1,0:T(8,128)(2,1)S(1)} async-done(((bf16[4,2,48,1024]{3,2,1,0:T(8,128)(2,1)}), bf16[4,2,48,1024]{3,2,1,0:T(8,128)(2,1)S(1)}, u32[]{:S(2)}, u32[]{:S(2)}) %all-to-all-start) | async-done | bytes 786464 | tf_op jit(solution)/shard_map/all_to_all | solution.py:13
  122.0 8.2 %collective-permute-done = bf16[512,1024]{1,0:T(8,128)(2,1)} collective-permute-done((bf16[512,1024]{1,0:T(8,128)(2,1)}, bf16[512,1024]{1,0:T(8,128)(2,1)}, u32[]{:S(2)}, u32[]{:S(2)}) %collective-permute-start) | collective-permute-done | bytes 1048608 | tf_op jit(solution)/shard_map/ppermute | solution.py:23
  132.8 5.7 %all_to_all.58 = bf16[2,2,96,1024]{3,2,1,0:T(8,128)(2,1)S(1)} all-to-all(bf16[2,2,96,1024]{3,2,1,0:T(8,128)(2,1)S(1)} %bitcast.61), channel_id=1, replica_groups=mesh['y'=4,'z1'=4,'z0'=2,'x'=4,'h'=2,'c'=2] {'c'}, dimensions={0} | all-to-all | bytes 1572864 | tf_op jit(solution)/shard_map/all_to_all | solution.py:13
  139.6 6.3 %collective-permute-start.1 = (bf16[2,96,1024]{2,1,0:T(8,128)(2,1)}, bf16[2,96,1024]{2,1,0:T(8,128)(2,1)S(1)}, u32[]{:S(2)}, u32[]{:S(2)}) collective-permute-start(bf16[2,96,1024]{2,1,0:T(8,128)(2,1)} %reduce_sum.51), channel_id=1, source_target_pairs={{0,2},{2,0},{1,3},{3,1},{4,6},{6,4},{5,7},{7,5},{8,10},{10,8},{9,1... | collective-permute-start | bytes 1179656 | tf_op jit(solution)/shard_map/ppermute | solution.py:27
  148.8 4.0 %all-to-all-start.6 = ((bf16[4,2,48,1024]{3,2,1,0:T(8,128)(2,1)}), bf16[4,2,48,1024]{3,2,1,0:T(8,128)(2,1)S(1)}, u32[]{:S(2)}, u32[]{:S(2)}) async-start(bf16[4,2,48,1024]{3,2,1,0:T(8,128)(2,1)} %bitcast.51), calls=%async_computation.6 | async-start | bytes 1572864 | tf_op jit(solution)/shard_map/all_to_all | solution.py:13
  156.2 8.1 %all-to-all-done.6 = bf16[4,2,48,1024]{3,2,1,0:T(8,128)(2,1)S(1)} async-done(((bf16[4,2,48,1024]{3,2,1,0:T(8,128)(2,1)}), bf16[4,2,48,1024]{3,2,1,0:T(8,128)(2,1)S(1)}, u32[]{:S(2)}, u32[]{:S(2)}) %all-to-all-start.6) | async-done | bytes 786464 | tf_op jit(solution)/shard_map/all_to_all | solution.py:13
  165.2 5.3 %all-to-all-start.3 = ((bf16[2,2,96,1024]{3,2,1,0:T(8,128)(2,1)}), bf16[2,2,96,1024]{3,2,1,0:T(8,128)(2,1)S(1)}, u32[]{:S(2)}, u32[]{:S(2)}) async-start(bf16[2,2,96,1024]{3,2,1,0:T(8,128)(2,1)} %broadcast_in_dim.18), calls=%async_computation.3 | async-start | bytes 1572864 | tf_op jit(solution)/shard_map/all_to_all | solution.py:13
  173.1 3.5 %all-to-all-start.7 = ((bf16[4,2,48,1024]{3,2,1,0:T(8,128)(2,1)}), bf16[4,2,48,1024]{3,2,1,0:T(8,128)(2,1)S(1)}, u32[]{:S(2)}, u32[]{:S(2)}) async-start(bf16[4,2,48,1024]{3,2,1,0:T(8,128)(2,1)} %broadcast_in_dim.21), calls=%async_computation.7 | async-start | bytes 1572864 | tf_op jit(solution)/shard_map/all_to_all | solution.py:13
  176.7 11.9 %all-to-all-done.7 = bf16[4,2,48,1024]{3,2,1,0:T(8,128)(2,1)S(1)} async-done(((bf16[4,2,48,1024]{3,2,1,0:T(8,128)(2,1)}), bf16[4,2,48,1024]{3,2,1,0:T(8,128)(2,1)S(1)}, u32[]{:S(2)}, u32[]{:S(2)}) %all-to-all-start.7) | async-done | bytes 786464 | tf_op jit(solution)/shard_map/all_to_all | solution.py:13
  196.0 8.8 %collective-permute-done.4 = bf16[256,1024]{1,0:T(8,128)(2,1)S(1)} collective-permute-done((bf16[256,1024]{1,0:T(8,128)(2,1)S(1)}, bf16[256,1024]{1,0:T(8,128)(2,1)S(1)}, u32[]{:S(2)}, u32[]{:S(2)}) %collective-permute-start.4) | collective-permute-done | bytes 524320 | tf_op jit(solution)/shard_map/ppermute | solution.py:23
  207.2 32.7 %all_to_all.59 = bf16[16,32,1024]{2,1,0:T(8,128)(2,1)S(1)} all-to-all(bf16[16,32,1024]{2,1,0:T(8,128)(2,1)S(1)} %bitcast.55), channel_id=1, replica_groups=mesh['y'=4,'z1'=4,'z0'=2,'x'=4,'h'=2,'c'=2] {'y','z1'}, dimensions={0} | all-to-all | bytes 2097152 | tf_op jit(solution)/shard_map/all_to_all | solution.py:13
  240.9 32.2 %all_to_all.60 = bf16[16,32,1024]{2,1,0:T(8,128)(2,1)S(1)} all-to-all(bf16[16,32,1024]{2,1,0:T(8,128)(2,1)S(1)} %broadcast_in_dim.22), channel_id=1, replica_groups=mesh['y'=4,'z1'=4,'z0'=2,'x'=4,'h'=2,'c'=2] {'y','z1'}, dimensions={0} | all-to-all | bytes 2097152 | tf_op jit(solution)/shard_map/all_to_all | solution.py:13
  273.2 5.2 %collective-permute-start.6 = (bf16[256,1024]{1,0:T(8,128)(2,1)S(1)}, bf16[256,1024]{1,0:T(8,128)(2,1)S(1)}, u32[]{:S(2)}, u32[]{:S(2)}) collective-permute-start(bf16[256,1024]{1,0:T(8,128)(2,1)S(1)} %bitcast.70), channel_id=1, source_target_pairs={{0,16},{16,32},{32,48},{48,64},{64,80},{80,96},{96,112},{112,0},{1... | collective-permute-start | bytes 1572872 | tf_op jit(solution)/shard_map/ppermute | solution.py:23
  281.8 8.2 %collective-permute-done.6 = bf16[256,1024]{1,0:T(8,128)(2,1)S(1)} collective-permute-done((bf16[256,1024]{1,0:T(8,128)(2,1)S(1)}, bf16[256,1024]{1,0:T(8,128)(2,1)S(1)}, u32[]{:S(2)}, u32[]{:S(2)}) %collective-permute-start.6) | collective-permute-done | bytes 524320 | tf_op jit(solution)/shard_map/ppermute | solution.py:23
  291.8 17.2 %all_to_all.61 = f32[16,1,192]{2,1,0:T(1,128)S(1)} all-to-all(f32[16,1,192]{2,1,0:T(1,128)S(1)} %broadcast_in_dim.23), channel_id=1, replica_groups=mesh['y'=4,'z1'=4,'z0'=2,'x'=4,'h'=2,'c'=2] {'x','h','c'}, dimensions={0} | all-to-all | bytes 24576 | tf_op jit(solution)/shard_map/all_to_all | solution.py:13
  (65 shorter events, 43.3 us)
Async XLA Ops:
  0.6 3.6 %copy-start.2 = (bf16[48,4096]{1,0:T(8,128)(2,1)S(1)}, bf16[48,4096]{1,0:T(8,128)(2,1)}, u32[]{:S(2)}) copy-start(bf16[48,4096]{1,0:T(8,128)(2,1)} %param.13) | copy-start | bytes 1179652
  15.3 16.1 %collective-permute-start.2 = (bf16[2,48,1024]{2,1,0:T(8,128)(2,1)S(1)}, bf16[2,48,1024]{2,1,0:T(8,128)(2,1)S(1)}, u32[]{:S(2)}, u32[]{:S(2)}) collective-permute-start(bf16[2,48,1024]{2,1,0:T(8,128)(2,1)S(1)} %constant_dynamic-update-slice_fusion.2), channel_id=1, source_target_pairs={{0,2},{2,0},{1,3},{3,1},{4,6},{6,4},{5,7},{7,5},{8,10},{10,8},{9,1... | collective-permute-start | bytes 589832 | tf_op jit(solution)/shard_map/ppermute | solution.py:27
  31.4 9.1 %copy-start.6 = (bf16[1024,32]{0,1:T(8,128)(2,1)S(1)}, bf16[1024,32]{0,1:T(8,128)(2,1)}, u32[]{:S(2)}) copy-start(bf16[1024,32]{0,1:T(8,128)(2,1)} %param.9) | copy-start | bytes 196612
  31.6 44.6 %copy-start.7 = (bf16[32,1024]{1,0:T(8,128)(2,1)S(1)}, bf16[32,1024]{1,0:T(8,128)(2,1)}, u32[]{:S(2)}) copy-start(bf16[32,1024]{1,0:T(8,128)(2,1)} %param.10) | copy-start | bytes 196612
  76.2 13.0 %copy-start.4 = (bf16[48,1024]{1,0:T(8,128)(2,1)S(1)}, bf16[48,1024]{1,0:T(8,128)(2,1)}, u32[]{:S(2)}) copy-start(bf16[48,1024]{1,0:T(8,128)(2,1)} %param.12) | copy-start | bytes 294916
  76.2 13.0 %copy-start.5 = (bf16[48,1024]{1,0:T(8,128)(2,1)S(1)}, bf16[48,1024]{1,0:T(8,128)(2,1)}, u32[]{:S(2)}) copy-start(bf16[48,1024]{1,0:T(8,128)(2,1)} %param.7) | copy-start | bytes 294916
  77.3 30.7 %all-to-all-start.5 = ((bf16[16,32,1024]{2,1,0:T(8,128)(2,1)}), bf16[16,32,1024]{2,1,0:T(8,128)(2,1)S(1)}, u32[]{:S(2)}, u32[]{:S(2)}) async-start(bf16[16,32,1024]{2,1,0:T(8,128)(2,1)} %broadcast_in_dim.20), calls=%async_computation.5 | async-start | bytes 2097152 | tf_op jit(solution)/shard_map/all_to_all | solution.py:13
  83.9 46.3 %collective-permute-start = (bf16[512,1024]{1,0:T(8,128)(2,1)}, bf16[512,1024]{1,0:T(8,128)(2,1)}, u32[]{:S(2)}, u32[]{:S(2)}) collective-permute-start(bf16[512,1024]{1,0:T(8,128)(2,1)} %bitcast.5), channel_id=1, source_target_pairs={{0,112},{16,0},{32,16},{48,32},{64,48},{80,64},{96,80},{112,96},{1... | collective-permute-start | bytes 3145736 | tf_op jit(solution)/shard_map/ppermute | solution.py:23
  109.0 12.4 %all-to-all-start = ((bf16[4,2,48,1024]{3,2,1,0:T(8,128)(2,1)}), bf16[4,2,48,1024]{3,2,1,0:T(8,128)(2,1)S(1)}, u32[]{:S(2)}, u32[]{:S(2)}) async-start(bf16[4,2,48,1024]{3,2,1,0:T(8,128)(2,1)} %broadcast_in_dim.16), calls=%async_computation | async-start | bytes 1572864 | tf_op jit(solution)/shard_map/all_to_all | solution.py:13
  113.0 32.9 %collective-permute-start.3 = (bf16[512,1024]{1,0:T(8,128)(2,1)S(1)}, bf16[512,1024]{1,0:T(8,128)(2,1)}, u32[]{:S(2)}, u32[]{:S(2)}) collective-permute-start(bf16[512,1024]{1,0:T(8,128)(2,1)S(1)} %bitcast.53), channel_id=1, source_target_pairs={{0,16},{16,32},{32,48},{48,64},{64,80},{80,96},{96,112},{112,0},{1... | collective-permute-start | bytes 3145736 | tf_op jit(solution)/shard_map/ppermute | solution.py:23
  116.5 5.5 %copy-start = (bf16[2,4,48,1024]{3,2,1,0:T(8,128)(2,1)}, bf16[2,4,48,1024]{3,2,1,0:T(8,128)(2,1)S(1)}, u32[]{:S(2)}) copy-start(bf16[2,4,48,1024]{3,2,1,0:T(8,128)(2,1)S(1)} %copy.30) | copy-start | bytes 2359300
  139.6 16.5 %collective-permute-start.1 = (bf16[2,96,1024]{2,1,0:T(8,128)(2,1)}, bf16[2,96,1024]{2,1,0:T(8,128)(2,1)S(1)}, u32[]{:S(2)}, u32[]{:S(2)}) collective-permute-start(bf16[2,96,1024]{2,1,0:T(8,128)(2,1)} %reduce_sum.51), channel_id=1, source_target_pairs={{0,2},{2,0},{1,3},{3,1},{4,6},{6,4},{5,7},{7,5},{8,10},{10,8},{9,1... | collective-permute-start | bytes 1179656 | tf_op jit(solution)/shard_map/ppermute | solution.py:27
  147.8 8.3 %copy-start.1 = (bf16[2,96,1024]{2,1,0:T(8,128)(2,1)S(1)}, bf16[2,96,1024]{2,1,0:T(8,128)(2,1)}, u32[]{:S(2)}) copy-start(bf16[2,96,1024]{2,1,0:T(8,128)(2,1)} %reduce_sum.51) | copy-start | bytes 1179652
  148.8 15.5 %all-to-all-start.6 = ((bf16[4,2,48,1024]{3,2,1,0:T(8,128)(2,1)}), bf16[4,2,48,1024]{3,2,1,0:T(8,128)(2,1)S(1)}, u32[]{:S(2)}, u32[]{:S(2)}) async-start(bf16[4,2,48,1024]{3,2,1,0:T(8,128)(2,1)} %bitcast.51), calls=%async_computation.6 | async-start | bytes 1572864 | tf_op jit(solution)/shard_map/all_to_all | solution.py:13
  165.2 6.9 %all-to-all-start.3 = ((bf16[2,2,96,1024]{3,2,1,0:T(8,128)(2,1)}), bf16[2,2,96,1024]{3,2,1,0:T(8,128)(2,1)S(1)}, u32[]{:S(2)}, u32[]{:S(2)}) async-start(bf16[2,2,96,1024]{3,2,1,0:T(8,128)(2,1)} %broadcast_in_dim.18), calls=%async_computation.3 | async-start | bytes 1572864 | tf_op jit(solution)/shard_map/all_to_all | solution.py:13
  173.1 15.5 %all-to-all-start.7 = ((bf16[4,2,48,1024]{3,2,1,0:T(8,128)(2,1)}), bf16[4,2,48,1024]{3,2,1,0:T(8,128)(2,1)S(1)}, u32[]{:S(2)}, u32[]{:S(2)}) async-start(bf16[4,2,48,1024]{3,2,1,0:T(8,128)(2,1)} %broadcast_in_dim.21), calls=%async_computation.7 | async-start | bytes 1572864 | tf_op jit(solution)/shard_map/all_to_all | solution.py:13
  189.5 15.4 %collective-permute-start.4 = (bf16[256,1024]{1,0:T(8,128)(2,1)S(1)}, bf16[256,1024]{1,0:T(8,128)(2,1)S(1)}, u32[]{:S(2)}, u32[]{:S(2)}) collective-permute-start(bf16[256,1024]{1,0:T(8,128)(2,1)S(1)} %get-tuple-element.6), channel_id=1, source_target_pairs={{0,16},{16,32},{32,48},{48,64},{64,80},{80,96},{96,112},{112,0},{1... | collective-permute-start | bytes 1572872 | tf_op jit(solution)/shard_map/ppermute | solution.py:23
  192.9 13.9 %collective-permute-start.5 = (bf16[256,1024]{1,0:T(8,128)(2,1)S(1)}, bf16[256,1024]{1,0:T(8,128)(2,1)S(1)}, u32[]{:S(2)}, u32[]{:S(2)}) collective-permute-start(bf16[256,1024]{1,0:T(8,128)(2,1)S(1)} %get-tuple-element.7), channel_id=1, source_target_pairs={{0,112},{16,0},{32,16},{48,32},{64,48},{80,64},{96,80},{112,96},{1... | collective-permute-start | bytes 1572872 | tf_op jit(solution)/shard_map/ppermute | solution.py:23
  207.2 32.9 %copy-start.3 = (f32[32,1024]{1,0:T(8,128)S(1)}, f32[32,1024]{1,0:T(8,128)}, u32[]{:S(2)}) copy-start(f32[32,1024]{1,0:T(8,128)} %param.11) | copy-start | bytes 393220
  273.2 16.8 %collective-permute-start.6 = (bf16[256,1024]{1,0:T(8,128)(2,1)S(1)}, bf16[256,1024]{1,0:T(8,128)(2,1)S(1)}, u32[]{:S(2)}, u32[]{:S(2)}) collective-permute-start(bf16[256,1024]{1,0:T(8,128)(2,1)S(1)} %bitcast.70), channel_id=1, source_target_pairs={{0,16},{16,32},{32,48},{48,64},{64,80},{80,96},{96,112},{112,0},{1... | collective-permute-start | bytes 1572872 | tf_op jit(solution)/shard_map/ppermute | solution.py:23
  278.4 12.7 %collective-permute-start.7 = (bf16[256,1024]{1,0:T(8,128)(2,1)S(1)}, bf16[256,1024]{1,0:T(8,128)(2,1)S(1)}, u32[]{:S(2)}, u32[]{:S(2)}) collective-permute-start(bf16[256,1024]{1,0:T(8,128)(2,1)S(1)} %bitcast.69), channel_id=1, source_target_pairs={{0,112},{16,0},{32,16},{48,32},{64,48},{80,64},{96,80},{112,96},{1... | collective-permute-start | bytes 1572872 | tf_op jit(solution)/shard_map/ppermute | solution.py:23

commit v3 on v2

--- a/solution.py
+++ b/solution.py
@@ -49,41 +49,55 @@
     peers = lax.axis_size(PEERS)
     row_count = lax.axis_size("x")
     rows_own, width = eigvals.shape
-    parity, side = lax.axis_index("z0"), lax.axis_index("h")
+    parity = lax.axis_index("z0")
     flat = (peers * rows_own, width)
 
-    split = jnp.stack([query_in, train_in])
-    rows = split.shape[1]
-    split = split.reshape(2, rows, peers, 2 * row_count, -1)
+    with jax.named_scope("panel_in"):
+        panel_in = gather(in_basis, PEERS).reshape(flat)
+    with jax.named_scope("near_in"):
+        panel_in_other = shift(panel_in, 1)
+    basis_rows, panel_in = lax.optimization_barrier((out_basis.T, panel_in))
+    with jax.named_scope("panel_out"):
+        panel_out = gather(basis_rows, PEERS).reshape(flat[0], -1)
+    with jax.named_scope("near_out"):
+        panel_out_other = shift(panel_out, -1)
 
-    def pick(which):
-        index = which * row_count + lax.axis_index("x")
-        part = lax.dynamic_index_in_dim(split, index, 3, keepdims=False)
-        return part.reshape(2, rows, -1)
+    def pick(tokens):
+        split = tokens.T.reshape(peers, 2 * row_count, -1, tokens.shape[0])
 
-    picked = jnp.concatenate([pick(parity), pick(1 - parity)], axis=2)
-    far = swap(picked, "h")
-    pair = jnp.where(side == 0, jnp.stack([picked, far]), jnp.stack([far, picked]))
-    near = gather(pair, "c")
-    tok_in = join_tokens(near.transpose(1, 0, 2, 3, 4).reshape((-1,) + near.shape[2:]))
-    tok_out = join_tokens(gather(jnp.stack([query_out, train_out]), "x"))
+        def part(which):
+            index = which * row_count + lax.axis_index("x")
+            found = lax.dynamic_index_in_dim(split, index, 1, keepdims=False)
+            return found.reshape(-1, tokens.shape[0])
 
-    panel_in = gather(in_basis, PEERS).reshape(flat)
-    panel_out = gather(out_basis.T, PEERS).reshape(flat[0], -1)
-    panel_in_other = shift(panel_in, 1)
-    panel_out_other = shift(panel_out, -1)
+        return jnp.concatenate([part(parity), part(1 - parity)], axis=0).T
+
+    def both(block, axis):
+        other = swap(block, axis)
+        first = lax.axis_index(axis) == 0
+        return jnp.where(first, jnp.stack([block, other]), jnp.stack([other, block]))
+
+    with jax.named_scope("pick"):
+        picked = jnp.stack([pick(query_in), pick(train_in)])
+    with jax.named_scope("tok_in"):
+        tok_in = both(both(picked, "c"), "h")
+        tok_in = join_tokens(tok_in.reshape((-1,) + picked.shape))
+    with jax.named_scope("tok_out"):
+        tok_out = join_tokens(gather(jnp.stack([query_out, train_out]), "x"))
 
     half = flat[0]
-    inr = dot(tok_in[..., :half], panel_in, ((2,), (0,)))
-    inr = inr + dot(tok_in[..., half:], panel_in_other, ((2,), (0,)))
-    inr = total(exchange(split_tokens(inr.astype(bf16), row_count), "x")).astype(bf16)
-    inr = join_tokens(gather(inr, "x"))
+    with jax.named_scope("inr"):
+        inr = dot(tok_in[..., :half], panel_in, ((2,), (0,)))
+        inr = inr + dot(tok_in[..., half:], panel_in_other, ((2,), (0,)))
+        inr = total(exchange(split_tokens(inr.astype(bf16), row_count), "x")).astype(bf16)
+        inr = join_tokens(gather(inr, "x"))
 
-    panels = jnp.concatenate([panel_out, panel_out_other], axis=0)
-    rot = dot(tok_out, panels, ((2,), (1,))).astype(bf16)
-    rot = total(exchange(split_tokens(rot, 2), "c")).astype(bf16)
-    rot = (rot.astype(f32) + swap(rot, "h").astype(f32)).astype(bf16)
-    rot = join_tokens(gather(rot, "c"))
+    with jax.named_scope("rot"):
+        panels = jnp.concatenate([panel_out, panel_out_other], axis=0)
+        rot = dot(tok_out, panels, ((2,), (1,))).astype(bf16)
+        rot = total(exchange(split_tokens(rot, 2), "c")).astype(bf16)
+        rot = (rot.astype(f32) + swap(rot, "h").astype(f32)).astype(bf16)
+        rot = join_tokens(gather(rot, "c"))
 
     partial_grad = dot(rot[0], inr[0], ((0,), (0,))).astype(bf16)
     own, other = partial_grad[:half], partial_grad[half:]

time: 312 us -> 292 us (0.936)
  waiting for transfers between devices: 84.3 us -> 58.7 us
  blocking collectives: 132 us -> 151 us
  starting transfers between devices: 61.8 us -> 52.6 us
  local copies, waits for them, and re-layouts: 20.5 us -> 17.2 us
    all_to_all x5 -> x4, waiting for transfers between devices: 45 us -> 18.5 us  [exchange(): return lax.all_to_all(blocks, axes, 0, 0, tiled=True)]
    all_to_all x6, blocking collectives: 132 us -> 151 us  [exchange(): return lax.all_to_all(blocks, axes, 0, 0, tiled=True)]
    all_to_all x5 -> x4, starting transfers between devices: 23.4 us -> 18.3 us  [exchange(): return lax.all_to_all(blocks, axes, 0, 0, tiled=True)]
    another operation x3 -> x0, local copies, waits for them, and re-layouts: 4.82 us -> none  [per_device(): split = jnp.stack([query_in, train_in])]
    ppermute x2 -> x3, waiting for transfers between devices: 11.1 us -> 15.7 us  [swap(): return lax.ppermute(block, axis, [(0, 1), (1, 0)])]
    reshape x2 -> x6, local copies, waits for them, and re-layouts: 0.6 us -> 4.44 us  [the longest x2 3.67 us: pick(): split = tokens.T.reshape(peers, 2 * row_count, -1, tokens.shape[0])]
    ppermute x6, waiting for transfers between devices: 28.2 us -> 24.5 us  [shift(): lax.ppermute(block, ('z1', 'z0'), [(i, (i + step) % count) for i in range...]
    ppermute x6, starting transfers between devices: 23.8 us -> 20.6 us  [shift(): lax.ppermute(block, ('z1', 'z0'), [(i, (i + step) % count) for i in range...]
  transfers between devices with their start and end apart: 13 -> 13, of which waited for: 12 -> 9; matrix products, arithmetic and copies ran while one was open for 3% -> 6% of each run, Pallas kernels for 0% -> 0%
where the time goes in v3:
time: 292 us; the launch traced here: 290 us
  blocking collectives  151 us (52%)
  waiting for transfers between devices  58.7 us (20%)
  starting transfers between devices  52.6 us (18%)
  local copies, waits for them, and re-layouts  17.2 us (6%)
  matrix products  6.34 us (2%)
    all_to_all x6, blocking collectives, exchange(): return lax.all_to_all(blocks, axes, 0, 0, tiled=True)  151 us
    ppermute x6, waiting for transfers between devices, shift(): lax.ppermute(block, ('z1', 'z0'), [(i, (i + step) % count) for i in range...  24.5 us
    ppermute x6, starting transfers between devices, shift(): lax.ppermute(block, ('z1', 'z0'), [(i, (i + step) % count) for i in range...  20.6 us
    all_to_all x4, waiting for transfers between devices, exchange(): return lax.all_to_all(blocks, axes, 0, 0, tiled=True)  18.5 us
    all_to_all x4, starting transfers between devices, exchange(): return lax.all_to_all(blocks, axes, 0, 0, tiled=True)  18.3 us
    ppermute x3, waiting for transfers between devices, swap(): return lax.ppermute(block, axis, [(0, 1), (1, 0)])  15.7 us
    ppermute x3, starting transfers between devices, swap(): return lax.ppermute(block, axis, [(0, 1), (1, 0)])  13.6 us
    dynamic_slice x1, local copies, waits for them, and re-layouts, part(): found = lax.dynamic_index_in_dim(split, index, 1, keepdims=False)  7 us
  transfers between devices with their start and end apart: 13, of which 9 were waited for; matrix products, arithmetic and copies ran while one was open for 6% of the time, Pallas kernels for 0%

profile of v3, /device:TPU:1, one launch (start us, length us, event | category | flops | bytes accessed | tf_op | source)
XLA Modules:
  0.0 290.0 jit_solution(18381362627951794147)
XLA Ops:
  1.6 39.9 %all_to_all.51 = bf16[16,32,1024]{2,1,0:T(8,128)(2,1)S(1)} all-to-all(bf16[16,32,1024]{2,1,0:T(8,128)(2,1)S(1)} %broadcast_in_dim.15), channel_id=1, replica_groups=mesh['y'=4,'z1'=4,'z0'=2,'x'=4,'h'=2,'c'=2] {'y','z1'}, dimensions={0} | all-to-all | bytes 2097152 | tf_op jit(solution)/shard_map/panel_in/all_to_all | solution.py:13
  42.7 6.8 %all-to-all-start.2 = ((bf16[16,32,1024]{2,1,0:T(8,128)(2,1)}), bf16[16,32,1024]{2,1,0:T(8,128)(2,1)}, u32[]{:S(2)}, u32[]{:S(2)}) async-start(bf16[16,32,1024]{2,1,0:T(8,128)(2,1)} %broadcast_in_dim.16), calls=%async_computation.2 | async-start | bytes 2097152 | tf_op jit(solution)/shard_map/panel_out/all_to_all | solution.py:13
  53.2 7.0 %dynamic-slice_reduce_fusion.1 = (bf16[16,32,48]{1,0,2:T(8,128)(2,1)S(1)}, bf16[16,32,48]{1,0,2:T(8,128)(2,1)S(1)}, bf16[16,32,48]{1,0,2:T(8,128)(2,1)S(1)}, bf16[16,32,48]{1,0,2:T(8,128)(2,1)S(1)}) fusion(bf16[16,8,32,48]{2,1,0,3:T(8,128)(2,1)} %reshape.147, s32[]{:T(128)S(6)} %select_n.42, s32[]{:T(128)S(6)} %select_n.43, ...), kind=kLoop, calls=%fused_computation.29 | loop fusion | bytes 393224 | tf_op jit(solution)/shard_map/pick/jit(dynamic_index_in_dim)/dynamic_slice | solution.py:70
  61.1 4.0 %collective-permute-start.2 = (bf16[2,48,1024]{2,1,0:T(8,128)(2,1)S(1)}, bf16[2,48,1024]{2,1,0:T(8,128)(2,1)S(1)}, u32[]{:S(2)}, u32[]{:S(2)}) collective-permute-start(bf16[2,48,1024]{2,1,0:T(8,128)(2,1)S(1)} %get-tuple-element.22), channel_id=1, source_target_pairs={{0,1},{1,0},{2,3},{3,2},{4,5},{5,4},{6,7},{7,6},{8,9},{9,8},{10,11... | collective-permute-start | bytes 589832 | tf_op jit(solution)/shard_map/tok_in/ppermute | solution.py:27
  67.9 4.8 %collective-permute-start.3 = (bf16[2,2,48,1024]{3,2,1,0:T(8,128)(2,1)S(1)}, bf16[2,2,48,1024]{3,2,1,0:T(8,128)(2,1)S(1)}, u32[]{:S(2)}, u32[]{:S(2)}) collective-permute-start(bf16[2,2,48,1024]{3,2,1,0:T(8,128)(2,1)S(1)} %maximum_select_fusion.2), channel_id=1, source_target_pairs={{0,2},{2,0},{1,3},{3,1},{4,6},{6,4},{5,7},{7,5},{8,10},{10,8},{9,1... | collective-permute-start | bytes 1179656 | tf_op jit(solution)/shard_map/tok_in/ppermute | solution.py:27
  72.8 11.4 %collective-permute-done.3 = bf16[2,2,48,1024]{3,2,1,0:T(8,128)(2,1)S(1)} collective-permute-done((bf16[2,2,48,1024]{3,2,1,0:T(8,128)(2,1)S(1)}, bf16[2,2,48,1024]{3,2,1,0:T(8,128)(2,1)S(1)}, u32[]{:S(2)}, u32[]{:S(2)}) %collective-permute-start.3) | collective-permute-done | bytes 393248 | tf_op jit(solution)/shard_map/tok_in/ppermute | solution.py:27
  85.4 4.0 %all-to-all-start = ((bf16[4,2,48,1024]{3,2,1,0:T(8,128)(2,1)}), bf16[4,2,48,1024]{3,2,1,0:T(8,128)(2,1)S(1)}, u32[]{:S(2)}, u32[]{:S(2)}) async-start(bf16[4,2,48,1024]{3,2,1,0:T(8,128)(2,1)} %broadcast_in_dim.14), calls=%async_computation | async-start | bytes 1572864 | tf_op jit(solution)/shard_map/tok_out/all_to_all | solution.py:13
  89.4 4.9 %collective-permute-start = (bf16[512,1024]{1,0:T(8,128)(2,1)}, bf16[512,1024]{1,0:T(8,128)(2,1)}, u32[]{:S(2)}, u32[]{:S(2)}) collective-permute-start(bf16[512,1024]{1,0:T(8,128)(2,1)} %bitcast.6), channel_id=1, source_target_pairs={{0,112},{16,0},{32,16},{48,32},{64,48},{80,64},{96,80},{112,96},{1... | collective-permute-start | bytes 3145736 | tf_op jit(solution)/shard_map/near_out/ppermute | solution.py:23
  94.9 4.4 %collective-permute-done.4 = bf16[512,1024]{1,0:T(8,128)(2,1)} collective-permute-done((bf16[512,1024]{1,0:T(8,128)(2,1)S(1)}, bf16[512,1024]{1,0:T(8,128)(2,1)}, u32[]{:S(2)}, u32[]{:S(2)}) %collective-permute-start.4) | collective-permute-done | bytes 1048608 | tf_op jit(solution)/shard_map/near_in/ppermute | solution.py:23
  102.1 4.0 %all-to-all-start.5 = ((bf16[4,2,48,1024]{3,2,1,0:T(8,128)(2,1)}), bf16[4,2,48,1024]{3,2,1,0:T(8,128)(2,1)S(1)}, u32[]{:S(2)}, u32[]{:S(2)}) async-start(bf16[4,2,48,1024]{3,2,1,0:T(8,128)(2,1)} %bitcast.72), calls=%async_computation.5 | async-start | bytes 1572864 | tf_op jit(solution)/shard_map/inr/all_to_all | solution.py:13
  106.2 11.6 %all-to-all-done.5 = bf16[4,2,48,1024]{3,2,1,0:T(8,128)(2,1)S(1)} async-done(((bf16[4,2,48,1024]{3,2,1,0:T(8,128)(2,1)}), bf16[4,2,48,1024]{3,2,1,0:T(8,128)(2,1)S(1)}, u32[]{:S(2)}, u32[]{:S(2)}) %all-to-all-start.5) | async-done | bytes 786464 | tf_op jit(solution)/shard_map/inr/all_to_all | solution.py:13
  120.5 5.6 %all_to_all.52 = bf16[2,2,96,1024]{3,2,1,0:T(8,128)(2,1)S(1)} all-to-all(bf16[2,2,96,1024]{3,2,1,0:T(8,128)(2,1)S(1)} %bitcast.82), channel_id=1, replica_groups=mesh['y'=4,'z1'=4,'z0'=2,'x'=4,'h'=2,'c'=2] {'c'}, dimensions={0} | all-to-all | bytes 1572864 | tf_op jit(solution)/shard_map/rot/all_to_all | solution.py:13
  127.1 3.5 %all-to-all-start.6 = ((bf16[4,2,48,1024]{3,2,1,0:T(8,128)(2,1)}), bf16[4,2,48,1024]{3,2,1,0:T(8,128)(2,1)S(1)}, u32[]{:S(2)}, u32[]{:S(2)}) async-start(bf16[4,2,48,1024]{3,2,1,0:T(8,128)(2,1)} %broadcast_in_dim.18), calls=%async_computation.6 | async-start | bytes 1572864 | tf_op jit(solution)/shard_map/inr/all_to_all | solution.py:13
  130.8 4.8 %collective-permute-start.1 = (bf16[2,96,1024]{2,1,0:T(8,128)(2,1)S(1)}, bf16[2,96,1024]{2,1,0:T(8,128)(2,1)S(1)}, u32[]{:S(2)}, u32[]{:S(2)}) collective-permute-start(bf16[2,96,1024]{2,1,0:T(8,128)(2,1)S(1)} %reduce_sum.51), channel_id=1, source_target_pairs={{0,2},{2,0},{1,3},{3,1},{4,6},{6,4},{5,7},{7,5},{8,10},{10,8},{9,1... | collective-permute-start | bytes 1179656 | tf_op jit(solution)/shard_map/rot/ppermute | solution.py:27
  135.6 7.0 %all-to-all-done.6 = bf16[4,2,48,1024]{3,2,1,0:T(8,128)(2,1)S(1)} async-done(((bf16[4,2,48,1024]{3,2,1,0:T(8,128)(2,1)}), bf16[4,2,48,1024]{3,2,1,0:T(8,128)(2,1)S(1)}, u32[]{:S(2)}, u32[]{:S(2)}) %all-to-all-start.6) | async-done | bytes 786464 | tf_op jit(solution)/shard_map/inr/all_to_all | solution.py:13
  142.7 4.3 %collective-permute-done.1 = bf16[2,96,1024]{2,1,0:T(8,128)(2,1)S(1)} collective-permute-done((bf16[2,96,1024]{2,1,0:T(8,128)(2,1)S(1)}, bf16[2,96,1024]{2,1,0:T(8,128)(2,1)S(1)}, u32[]{:S(2)}, u32[]{:S(2)}) %collective-permute-start.1) | collective-permute-done | bytes 393248 | tf_op jit(solution)/shard_map/rot/ppermute | solution.py:27
  147.1 5.2 %all_to_all.53 = bf16[2,2,96,1024]{3,2,1,0:T(8,128)(2,1)S(1)} all-to-all(bf16[2,2,96,1024]{3,2,1,0:T(8,128)(2,1)S(1)} %broadcast_in_dim.17), channel_id=1, replica_groups=mesh['y'=4,'z1'=4,'z0'=2,'x'=4,'h'=2,'c'=2] {'c'}, dimensions={0} | all-to-all | bytes 1572864 | tf_op jit(solution)/shard_map/rot/all_to_all | solution.py:13
  155.6 4.1 %collective-permute-start.6 = (bf16[256,1024]{1,0:T(8,128)(2,1)S(1)}, bf16[256,1024]{1,0:T(8,128)(2,1)S(1)}, u32[]{:S(2)}, u32[]{:S(2)}) collective-permute-start(bf16[256,1024]{1,0:T(8,128)(2,1)S(1)} %get-tuple-element.13), channel_id=1, source_target_pairs={{0,112},{16,0},{32,16},{48,32},{64,48},{80,64},{96,80},{112,96},{1... | collective-permute-start | bytes 1572872 | tf_op jit(solution)/shard_map/ppermute | solution.py:23
  159.8 9.7 %collective-permute-done.5 = bf16[256,1024]{1,0:T(8,128)(2,1)S(1)} collective-permute-done((bf16[256,1024]{1,0:T(8,128)(2,1)S(1)}, bf16[256,1024]{1,0:T(8,128)(2,1)S(1)}, u32[]{:S(2)}, u32[]{:S(2)}) %collective-permute-start.5) | collective-permute-done | bytes 524320 | tf_op jit(solution)/shard_map/ppermute | solution.py:23
  171.7 47.3 %all_to_all.54 = bf16[16,32,1024]{2,1,0:T(8,128)(2,1)S(1)} all-to-all(bf16[16,32,1024]{2,1,0:T(8,128)(2,1)S(1)} %bitcast.76), channel_id=1, replica_groups=mesh['y'=4,'z1'=4,'z0'=2,'x'=4,'h'=2,'c'=2] {'y','z1'}, dimensions={0} | all-to-all | bytes 2097152 | tf_op jit(solution)/shard_map/all_to_all | solution.py:13
  219.9 31.9 %all_to_all.55 = bf16[16,32,1024]{2,1,0:T(8,128)(2,1)S(1)} all-to-all(bf16[16,32,1024]{2,1,0:T(8,128)(2,1)S(1)} %broadcast_in_dim.19), channel_id=1, replica_groups=mesh['y'=4,'z1'=4,'z0'=2,'x'=4,'h'=2,'c'=2] {'y','z1'}, dimensions={0} | all-to-all | bytes 2097152 | tf_op jit(solution)/shard_map/all_to_all | solution.py:13
  255.0 3.6 %collective-permute-start.8 = (bf16[256,1024]{1,0:T(8,128)(2,1)S(1)}, bf16[256,1024]{1,0:T(8,128)(2,1)S(1)}, u32[]{:S(2)}, u32[]{:S(2)}) collective-permute-start(bf16[256,1024]{1,0:T(8,128)(2,1)S(1)} %bitcast.92), channel_id=1, source_target_pairs={{0,112},{16,0},{32,16},{48,32},{64,48},{80,64},{96,80},{112,96},{1... | collective-permute-start | bytes 1572872 | tf_op jit(solution)/shard_map/ppermute | solution.py:23
  258.6 6.7 %collective-permute-done.7 = bf16[256,1024]{1,0:T(8,128)(2,1)S(1)} collective-permute-done((bf16[256,1024]{1,0:T(8,128)(2,1)S(1)}, bf16[256,1024]{1,0:T(8,128)(2,1)S(1)}, u32[]{:S(2)}, u32[]{:S(2)}) %collective-permute-start.7) | collective-permute-done | bytes 524320 | tf_op jit(solution)/shard_map/ppermute | solution.py:23
  267.9 21.5 %all_to_all.56 = f32[16,1,192]{2,1,0:T(1,128)S(1)} all-to-all(f32[16,1,192]{2,1,0:T(1,128)S(1)} %broadcast_in_dim.20), channel_id=1, replica_groups=mesh['y'=4,'z1'=4,'z0'=2,'x'=4,'h'=2,'c'=2] {'x','h','c'}, dimensions={0} | all-to-all | bytes 24576 | tf_op jit(solution)/shard_map/all_to_all | solution.py:13
  (61 shorter events, 30.9 us)
Async XLA Ops:
  0.6 40.9 %copy-start.5 = (bf16[1024,32]{0,1:T(8,128)(2,1)S(1)}, bf16[1024,32]{0,1:T(8,128)(2,1)}, u32[]{:S(2)}) copy-start(bf16[1024,32]{0,1:T(8,128)(2,1)} %param.9) | copy-start | bytes 196612
  41.5 8.0 %copy-start = (bf16[48,4096]{1,0:T(8,128)(2,1)S(1)}, bf16[48,4096]{1,0:T(8,128)(2,1)}, u32[]{:S(2)}) copy-start(bf16[48,4096]{1,0:T(8,128)(2,1)} %param.8) | copy-start | bytes 1179652
  42.7 8.1 %copy-start.1 = (bf16[48,4096]{1,0:T(8,128)(2,1)S(1)}, bf16[48,4096]{1,0:T(8,128)(2,1)}, u32[]{:S(2)}) copy-start(bf16[48,4096]{1,0:T(8,128)(2,1)} %param.13) | copy-start | bytes 1179652
  42.7 41.7 %all-to-all-start.2 = ((bf16[16,32,1024]{2,1,0:T(8,128)(2,1)}), bf16[16,32,1024]{2,1,0:T(8,128)(2,1)}, u32[]{:S(2)}, u32[]{:S(2)}) async-start(bf16[16,32,1024]{2,1,0:T(8,128)(2,1)} %broadcast_in_dim.16), calls=%async_computation.2 | async-start | bytes 2097152 | tf_op jit(solution)/shard_map/panel_out/all_to_all | solution.py:13
  53.2 19.5 %copy-start.3 = (bf16[48,1024]{1,0:T(8,128)(2,1)S(1)}, bf16[48,1024]{1,0:T(8,128)(2,1)}, u32[]{:S(2)}) copy-start(bf16[48,1024]{1,0:T(8,128)(2,1)} %param.12) | copy-start | bytes 294916
  60.2 12.5 %copy-start.4 = (bf16[48,1024]{1,0:T(8,128)(2,1)S(1)}, bf16[48,1024]{1,0:T(8,128)(2,1)}, u32[]{:S(2)}) copy-start(bf16[48,1024]{1,0:T(8,128)(2,1)} %param.7) | copy-start | bytes 294916
  61.1 6.8 %collective-permute-start.2 = (bf16[2,48,1024]{2,1,0:T(8,128)(2,1)S(1)}, bf16[2,48,1024]{2,1,0:T(8,128)(2,1)S(1)}, u32[]{:S(2)}, u32[]{:S(2)}) collective-permute-start(bf16[2,48,1024]{2,1,0:T(8,128)(2,1)S(1)} %get-tuple-element.22), channel_id=1, source_target_pairs={{0,1},{1,0},{2,3},{3,2},{4,5},{5,4},{6,7},{7,6},{8,9},{9,8},{10,11... | collective-permute-start | bytes 589832 | tf_op jit(solution)/shard_map/tok_in/ppermute | solution.py:27
  65.1 34.2 %collective-permute-start.4 = (bf16[512,1024]{1,0:T(8,128)(2,1)S(1)}, bf16[512,1024]{1,0:T(8,128)(2,1)}, u32[]{:S(2)}, u32[]{:S(2)}) collective-permute-start(bf16[512,1024]{1,0:T(8,128)(2,1)S(1)} %bitcast.74), channel_id=1, source_target_pairs={{0,16},{16,32},{32,48},{48,64},{64,80},{80,96},{96,112},{112,0},{1... | collective-permute-start | bytes 3145736 | tf_op jit(solution)/shard_map/near_in/ppermute | solution.py:23
  67.9 16.3 %collective-permute-start.3 = (bf16[2,2,48,1024]{3,2,1,0:T(8,128)(2,1)S(1)}, bf16[2,2,48,1024]{3,2,1,0:T(8,128)(2,1)S(1)}, u32[]{:S(2)}, u32[]{:S(2)}) collective-permute-start(bf16[2,2,48,1024]{3,2,1,0:T(8,128)(2,1)S(1)} %maximum_select_fusion.2), channel_id=1, source_target_pairs={{0,2},{2,0},{1,3},{3,1},{4,6},{6,4},{5,7},{7,5},{8,10},{10,8},{9,1... | collective-permute-start | bytes 1179656 | tf_op jit(solution)/shard_map/tok_in/ppermute | solution.py:27
  85.4 16.7 %all-to-all-start = ((bf16[4,2,48,1024]{3,2,1,0:T(8,128)(2,1)}), bf16[4,2,48,1024]{3,2,1,0:T(8,128)(2,1)S(1)}, u32[]{:S(2)}, u32[]{:S(2)}) async-start(bf16[4,2,48,1024]{3,2,1,0:T(8,128)(2,1)} %broadcast_in_dim.14), calls=%async_computation | async-start | bytes 1572864 | tf_op jit(solution)/shard_map/tok_out/all_to_all | solution.py:13
  89.4 28.5 %collective-permute-start = (bf16[512,1024]{1,0:T(8,128)(2,1)}, bf16[512,1024]{1,0:T(8,128)(2,1)}, u32[]{:S(2)}, u32[]{:S(2)}) collective-permute-start(bf16[512,1024]{1,0:T(8,128)(2,1)} %bitcast.6), channel_id=1, source_target_pairs={{0,112},{16,0},{32,16},{48,32},{64,48},{80,64},{96,80},{112,96},{1... | collective-permute-start | bytes 3145736 | tf_op jit(solution)/shard_map/near_out/ppermute | solution.py:23
  102.1 15.6 %all-to-all-start.5 = ((bf16[4,2,48,1024]{3,2,1,0:T(8,128)(2,1)}), bf16[4,2,48,1024]{3,2,1,0:T(8,128)(2,1)S(1)}, u32[]{:S(2)}, u32[]{:S(2)}) async-start(bf16[4,2,48,1024]{3,2,1,0:T(8,128)(2,1)} %bitcast.72), calls=%async_computation.5 | async-start | bytes 1572864 | tf_op jit(solution)/shard_map/inr/all_to_all | solution.py:13
  127.1 15.5 %all-to-all-start.6 = ((bf16[4,2,48,1024]{3,2,1,0:T(8,128)(2,1)}), bf16[4,2,48,1024]{3,2,1,0:T(8,128)(2,1)S(1)}, u32[]{:S(2)}, u32[]{:S(2)}) async-start(bf16[4,2,48,1024]{3,2,1,0:T(8,128)(2,1)} %broadcast_in_dim.18), calls=%async_computation.6 | async-start | bytes 1572864 | tf_op jit(solution)/shard_map/inr/all_to_all | solution.py:13
  130.8 16.1 %collective-permute-start.1 = (bf16[2,96,1024]{2,1,0:T(8,128)(2,1)S(1)}, bf16[2,96,1024]{2,1,0:T(8,128)(2,1)S(1)}, u32[]{:S(2)}, u32[]{:S(2)}) collective-permute-start(bf16[2,96,1024]{2,1,0:T(8,128)(2,1)S(1)} %reduce_sum.51), channel_id=1, source_target_pairs={{0,2},{2,0},{1,3},{3,1},{4,6},{6,4},{5,7},{7,5},{8,10},{10,8},{9,1... | collective-permute-start | bytes 1179656 | tf_op jit(solution)/shard_map/rot/ppermute | solution.py:27
  153.3 16.2 %collective-permute-start.5 = (bf16[256,1024]{1,0:T(8,128)(2,1)S(1)}, bf16[256,1024]{1,0:T(8,128)(2,1)S(1)}, u32[]{:S(2)}, u32[]{:S(2)}) collective-permute-start(bf16[256,1024]{1,0:T(8,128)(2,1)S(1)} %get-tuple-element.12), channel_id=1, source_target_pairs={{0,16},{16,32},{32,48},{48,64},{64,80},{80,96},{96,112},{112,0},{1... | collective-permute-start | bytes 1572872 | tf_op jit(solution)/shard_map/ppermute | solution.py:23
  155.6 15.6 %collective-permute-start.6 = (bf16[256,1024]{1,0:T(8,128)(2,1)S(1)}, bf16[256,1024]{1,0:T(8,128)(2,1)S(1)}, u32[]{:S(2)}, u32[]{:S(2)}) collective-permute-start(bf16[256,1024]{1,0:T(8,128)(2,1)S(1)} %get-tuple-element.13), channel_id=1, source_target_pairs={{0,112},{16,0},{32,16},{48,32},{64,48},{80,64},{96,80},{112,96},{1... | collective-permute-start | bytes 1572872 | tf_op jit(solution)/shard_map/ppermute | solution.py:23
  171.6 47.5 %copy-start.2 = (f32[32,1024]{1,0:T(8,128)S(1)}, f32[32,1024]{1,0:T(8,128)}, u32[]{:S(2)}) copy-start(f32[32,1024]{1,0:T(8,128)} %param.11) | copy-start | bytes 393220
  252.0 13.3 %collective-permute-start.7 = (bf16[256,1024]{1,0:T(8,128)(2,1)S(1)}, bf16[256,1024]{1,0:T(8,128)(2,1)S(1)}, u32[]{:S(2)}, u32[]{:S(2)}) collective-permute-start(bf16[256,1024]{1,0:T(8,128)(2,1)S(1)} %bitcast.93), channel_id=1, source_target_pairs={{0,16},{16,32},{32,48},{48,64},{64,80},{80,96},{96,112},{112,0},{1... | collective-permute-start | bytes 1572872 | tf_op jit(solution)/shard_map/ppermute | solution.py:23
  255.0 12.2 %collective-permute-start.8 = (bf16[256,1024]{1,0:T(8,128)(2,1)S(1)}, bf16[256,1024]{1,0:T(8,128)(2,1)S(1)}, u32[]{:S(2)}, u32[]{:S(2)}) collective-permute-start(bf16[256,1024]{1,0:T(8,128)(2,1)S(1)} %bitcast.92), channel_id=1, source_target_pairs={{0,112},{16,0},{32,16},{48,32},{64,48},{80,64},{96,80},{112,96},{1... | collective-permute-start | bytes 1572872 | tf_op jit(solution)/shard_map/ppermute | solution.py:23

commit v4 on v3

v4 whole, which is shorter than its diff:
```python
import jax
import jax.numpy as jnp
from jax import lax
from jax.sharding import Mesh, PartitionSpec as P

damping = 1.0
f32, bf16 = jnp.float32, jnp.bfloat16
PEERS = ("y", "z1")
COL = ("h", "c")


def exchange(blocks, axes):
    return lax.all_to_all(blocks, axes, 0, 0, tiled=True)


def gather(block, axes):
    count = lax.axis_size(axes)
    return exchange(jnp.broadcast_to(block[None], (count,) + block.shape), axes)


def shift(block, step):
    count = lax.axis_size(("z1", "z0"))
    return lax.ppermute(block, ("z1", "z0"), [(i, (i + step) % count) for i in range(count)])


def swap(block, axis):
    return lax.ppermute(block, axis, [(0, 1), (1, 0)])


def total(blocks):
    return jnp.sum(blocks.astype(f32), axis=0)


def split_tokens(partial, count):
    two, tokens, width = partial.shape
    return partial.reshape(two, count, tokens // count, width).transpose(1, 0, 2, 3)


def join_tokens(parts):
    count, two, rows, width = parts.shape
    return parts.transpose(1, 0, 2, 3).reshape(two, count * rows, width)


def dot(left, right, dims):
    return lax.dot_general(left, right, (dims, ((), ())), preferred_element_type=f32)


def per_device(query_out, query_in, out_basis, in_basis, eigvals, train_out, train_in):
    peers = lax.axis_size(PEERS)
    row_count = lax.axis_size("x")
    rows_own, width = eigvals.shape
    parity = lax.axis_index("z0")
    half = peers * rows_own

    panels = gather(jnp.concatenate([in_basis, out_basis.T], axis=0), PEERS)

    def pick(tokens):
        split = tokens.T.reshape(peers, 2 * row_count, -1, tokens.shape[0])

        def part(which):
            index = which * row_count + lax.axis_index("x")
            found = lax.dynamic_index_in_dim(split, index, 1, keepdims=False)
            return found.reshape(-1, tokens.shape[0])

        return jnp.concatenate([part(parity), part(1 - parity)], axis=0).T

    def both(block, axis, at):
        other = swap(block, axis)
        first = lax.axis_index(axis) == 0
        return jnp.where(
            first, jnp.stack([block, other], axis=at), jnp.stack([other, block], axis=at)
        )

    picked = jnp.stack([pick(query_in), pick(train_in)])
    pair = both(picked, "h", 0)
    tokens = jnp.stack([query_out, train_out])
    panels, pair, tokens = lax.optimization_barrier((panels, pair, tokens))
    panel_in = panels[:, :rows_own].reshape(half, width)
    panel_out = panels[:, rows_own:].reshape(half, -1)
    panel_in_other = shift(panel_in, 1)
    tok_in = both(pair, "c", 1)
    tok_in = join_tokens(tok_in.reshape((-1,) + picked.shape))
    tok_out = join_tokens(gather(tokens, ("z0", "x")))

    rot = dot(tok_out, panel_out, ((2,), (1,))).astype(bf16)
    rot = total(exchange(split_tokens(rot, 2), "c")).astype(bf16)
    rot = (rot.astype(f32) + swap(rot, "h").astype(f32)).astype(bf16)
    rot = join_tokens(gather(rot, "c"))

    inr = dot(tok_in[..., :half], panel_in, ((2,), (0,)))
    inr = inr + dot(tok_in[..., half:], panel_in_other, ((2,), (0,)))
    inr = total(exchange(split_tokens(inr.astype(bf16), row_count), "x")).astype(bf16)
    inr = join_tokens(gather(inr, ("z0", "x")))

    partial_grad = dot(rot[0], inr[0], ((0,), (0,))).astype(bf16)
    grad = total(exchange(partial_grad.reshape(peers, rows_own, width), PEERS))
    precond = grad / (eigvals + damping)

    shared = gather(precond.astype(bf16), PEERS).reshape(half, width)
    mixed = dot(rot[1], shared, ((1,), (0,)))
    partial_scores = jnp.sum(mixed * inr[1].astype(f32), axis=1)
    adders = ("x",) + COL
    blocks = jnp.broadcast_to(
        partial_scores.reshape(2, 1, -1), (2, lax.axis_size(adders), partial_scores.size // 2)
    )
    blocks = blocks.reshape(-1, 1, partial_scores.size // 2)
    scores = total(exchange(blocks, ("z0",) + adders)).reshape(-1)
    return precond, scores


def solution(mesh):
    groups, row_count, cols = mesh.devices.shape
    sizes = (4, groups // 8, 2, row_count, 2, cols // 2)
    fine = Mesh(mesh.devices.reshape(sizes), ("y", "z1", "z0", "x", "h", "c"))
    dp = ("y", "z1", "z0")
    by_rows, by_tokens = P(dp + ("x",), COL), P(dp + COL, None)
    in_specs = (
        by_rows,
        by_tokens,
        P(COL, dp + ("x",)),
        by_rows,
        by_rows,
        by_rows,
        by_tokens,
    )
    return jax.shard_map(
        per_device, mesh=fine, in_specs=in_specs, out_specs=(by_rows, P(dp)), check_vma=False
    )
```

time: 292 us -> 283 us (0.969)
  blocking collectives: 151 us -> 109 us
  waiting for transfers between devices: 58.7 us -> 89.4 us
  local copies, waits for them, and re-layouts: 17.2 us -> 22.7 us
    all_to_all x6 -> x5, blocking collectives: 151 us -> 109 us  [exchange(): return lax.all_to_all(blocks, axes, 0, 0, tiled=True)]
    ppermute x3, waiting for transfers between devices: 15.7 us -> 34 us  [swap(): return lax.ppermute(block, axis, [(0, 1), (1, 0)])]
    ppermute x6 -> x1, starting transfers between devices: 20.6 us -> 3.36 us  [shift(): lax.ppermute(block, ('z1', 'z0'), [(i, (i + step) % count) for i in range...]
    all_to_all x4, starting transfers between devices: 18.3 us -> 31.1 us  [exchange(): return lax.all_to_all(blocks, axes, 0, 0, tiled=True)]
    all_to_all x4, waiting for transfers between devices: 18.5 us -> 29.6 us  [exchange(): return lax.all_to_all(blocks, axes, 0, 0, tiled=True)]
    ppermute x3, starting transfers between devices: 13.6 us -> 18.8 us  [swap(): return lax.ppermute(block, axis, [(0, 1), (1, 0)])]
    ppermute x6 -> x1, waiting for transfers between devices: 24.5 us -> 25.8 us  [shift(): lax.ppermute(block, ('z1', 'z0'), [(i, (i + step) % count) for i in range...]
  transfers between devices with their start and end apart: 13 -> 8, of which waited for: 9 -> 7; matrix products, arithmetic and copies ran while one was open for 6% -> 6% of each run, Pallas kernels for 0% -> 0%
where the time goes in v4:
time: 283 us; the launch traced here: 282 us
  blocking collectives  109 us (39%)
  waiting for transfers between devices  89.4 us (32%)
  starting transfers between devices  53.3 us (19%)
  local copies, waits for them, and re-layouts  22.7 us (8%)
  matrix products  3.55 us (1%)
  other arithmetic  3 us (1%)
    all_to_all x5, blocking collectives, exchange(): return lax.all_to_all(blocks, axes, 0, 0, tiled=True)  109 us
    ppermute x3, waiting for transfers between devices, swap(): return lax.ppermute(block, axis, [(0, 1), (1, 0)])  34 us
    all_to_all x4, starting transfers between devices, exchange(): return lax.all_to_all(blocks, axes, 0, 0, tiled=True)  31.1 us
    all_to_all x4, waiting for transfers between devices, exchange(): return lax.all_to_all(blocks, axes, 0, 0, tiled=True)  29.6 us
    ppermute x1, waiting for transfers between devices, shift(): lax.ppermute(block, ('z1', 'z0'), [(i, (i + step) % count) for i in range...  25.8 us
    ppermute x3, starting transfers between devices, swap(): return lax.ppermute(block, axis, [(0, 1), (1, 0)])  18.8 us
    dynamic_slice x1, local copies, waits for them, and re-layouts, part(): found = lax.dynamic_index_in_dim(split, index, 1, keepdims=False)  8.16 us
  transfers between devices with their start and end apart: 8, of which 7 were waited for; matrix products, arithmetic and copies ran while one was open for 6% of the time, Pallas kernels for 0%

profile of v4, /device:TPU:1, one launch (start us, length us, event | category | flops | bytes accessed | tf_op | source)
XLA Modules:
  0.0 281.8 jit_solution(16261328488354855565)
XLA Ops:
  1.5 1.6 broadcast_in_dim.14
  3.1 14.1 %all-to-all-start = ((bf16[16,64,1024]{2,1,0:T(8,128)(2,1)}), bf16[16,64,1024]{2,1,0:T(8,128)(2,1)S(1)}, u32[]{:S(2)}, u32[]{:S(2)}) async-start(bf16[16,64,1024]{2,1,0:T(8,128)(2,1)} %broadcast_in_dim.14), calls=%async_computation | async-start | bytes 4194304 | tf_op jit(solution)/shard_map/all_to_all | solution.py:13
  17.3 2.4 reshape.80
  19.7 2.4 reshape.83
  22.1 8.2 %dynamic-slice_reduce_fusion.1 = (bf16[16,32,48]{1,0,2:T(8,128)(2,1)S(1)}, bf16[16,32,48]{1,0,2:T(8,128)(2,1)S(1)}, bf16[16,32,48]{1,0,2:T(8,128)(2,1)S(1)}, bf16[16,32,48]{1,0,2:T(8,128)(2,1)S(1)}) fusion(bf16[16,8,32,48]{2,1,0,3:T(8,128)(2,1)} %reshape.83, s32[]{:T(128)S(6)} %select_n.30, s32[]{:T(128)S(6)} %select_n.31, bf16[16,8,32,48]{2,1,0,3:T(8,128)(2,1)} %reshape.80), kind=kLoop, calls=%fused_computation.16 | loop fusion | bytes 393224 | tf_op jit(solution)/shard_map/jit(dynamic_index_in_dim)/dynamic_slice | solution.py:62
  31.2 4.8 %collective-permute-start = (bf16[2,48,1024]{2,1,0:T(8,128)(2,1)S(1)}, bf16[2,48,1024]{2,1,0:T(8,128)(2,1)S(1)}, u32[]{:S(2)}, u32[]{:S(2)}) collective-permute-start(bf16[2,48,1024]{2,1,0:T(8,128)(2,1)S(1)} %get-tuple-element.21), channel_id=1, source_target_pairs={{0,2},{2,0},{1,3},{3,1},{4,6},{6,4},{5,7},{7,5},{8,10},{10,8},{9,1... | collective-permute-start | bytes 589832 | tf_op jit(solution)/shard_map/ppermute | solution.py:27
  36.0 26.8 %collective-permute-done = bf16[2,48,1024]{2,1,0:T(8,128)(2,1)S(1)} collective-permute-done((bf16[2,48,1024]{2,1,0:T(8,128)(2,1)S(1)}, bf16[2,48,1024]{2,1,0:T(8,128)(2,1)S(1)}, u32[]{:S(2)}, u32[]{:S(2)}) %collective-permute-start) | collective-permute-done | bytes 196640 | tf_op jit(solution)/shard_map/ppermute | solution.py:27
  62.9 6.4 %all-to-all-done = bf16[16,64,1024]{2,1,0:T(8,128)(2,1)S(1)} async-done(((bf16[16,64,1024]{2,1,0:T(8,128)(2,1)}), bf16[16,64,1024]{2,1,0:T(8,128)(2,1)S(1)}, u32[]{:S(2)}, u32[]{:S(2)}) %all-to-all-start) | async-done | bytes 2097184 | tf_op jit(solution)/shard_map/all_to_all | solution.py:13
  70.7 6.6 %all-to-all-start.1 = ((bf16[8,2,48,1024]{3,2,1,0:T(8,128)(2,1)}), bf16[8,2,48,1024]{3,2,1,0:T(8,128)(2,1)}, u32[]{:S(2)}, u32[]{:S(2)}) async-start(bf16[8,2,48,1024]{3,2,1,0:T(8,128)(2,1)} %broadcast_in_dim.15), calls=%async_computation.1 | async-start | bytes 3145728 | tf_op jit(solution)/shard_map/all_to_all | solution.py:13
  78.5 3.4 %collective-permute-start.3 = (bf16[512,1024]{1,0:T(8,128)(2,1)S(1)}, bf16[512,1024]{1,0:T(8,128)(2,1)S(1)}, u32[]{:S(2)}, u32[]{:S(2)}) collective-permute-start(bf16[512,1024]{1,0:T(8,128)(2,1)S(1)} %bitcast.70), channel_id=1, source_target_pairs={{0,16},{16,32},{32,48},{48,64},{64,80},{80,96},{96,112},{112,0},{1... | collective-permute-start | bytes 3145736 | tf_op jit(solution)/shard_map/ppermute | solution.py:23
  81.9 5.1 %collective-permute-start.2 = (bf16[2,2,48,1024]{3,2,1,0:T(8,128)(2,1)S(1)}, bf16[2,2,48,1024]{3,2,1,0:T(8,128)(2,1)S(1)}, u32[]{:S(2)}, u32[]{:S(2)}) collective-permute-start(bf16[2,2,48,1024]{3,2,1,0:T(8,128)(2,1)S(1)} %maximum_select_fusion.1), channel_id=1, source_target_pairs={{0,1},{1,0},{2,3},{3,2},{4,5},{5,4},{6,7},{7,6},{8,9},{9,8},{10,11... | collective-permute-start | bytes 1179656 | tf_op jit(solution)/shard_map/ppermute | solution.py:27
  89.0 25.8 %collective-permute-done.3 = bf16[512,1024]{1,0:T(8,128)(2,1)S(1)} collective-permute-done((bf16[512,1024]{1,0:T(8,128)(2,1)S(1)}, bf16[512,1024]{1,0:T(8,128)(2,1)S(1)}, u32[]{:S(2)}, u32[]{:S(2)}) %collective-permute-start.3) | collective-permute-done | bytes 1048608 | tf_op jit(solution)/shard_map/ppermute | solution.py:23
  116.3 1.6 copy.11
  119.1 7.0 %all_to_all.45 = bf16[2,2,192,512]{3,2,1,0:T(8,128)(2,1)S(1)} all-to-all(bf16[2,2,192,512]{3,2,1,0:T(8,128)(2,1)S(1)} %bitcast.75), channel_id=1, replica_groups=mesh['y'=4,'z1'=4,'z0'=2,'x'=4,'h'=2,'c'=2] {'c'}, dimensions={0} | all-to-all | bytes 1572864 | tf_op jit(solution)/shard_map/all_to_all | solution.py:13
  126.1 4.2 %all-to-all-start.4 = ((bf16[4,2,48,1024]{3,2,1,0:T(8,128)(2,1)}), bf16[4,2,48,1024]{3,2,1,0:T(8,128)(2,1)S(1)}, u32[]{:S(2)}, u32[]{:S(2)}) async-start(bf16[4,2,48,1024]{3,2,1,0:T(8,128)(2,1)} %bitcast.67), calls=%async_computation.4 | async-start | bytes 1572864 | tf_op jit(solution)/shard_map/all_to_all | solution.py:13
  130.5 8.9 %collective-permute-start.1 = (bf16[2,192,512]{2,1,0:T(8,128)(2,1)S(1)}, bf16[2,192,512]{2,1,0:T(8,128)(2,1)S(1)}, u32[]{:S(2)}, u32[]{:S(2)}) collective-permute-start(bf16[2,192,512]{2,1,0:T(8,128)(2,1)S(1)} %reduce_sum.51), channel_id=1, source_target_pairs={{0,2},{2,0},{1,3},{3,1},{4,6},{6,4},{5,7},{7,5},{8,10},{10,8},{9,1... | collective-permute-start | bytes 1179656 | tf_op jit(solution)/shard_map/ppermute | solution.py:27
  139.4 2.6 all-to-all-done.4
  142.2 6.1 %collective-permute-done.1 = bf16[2,192,512]{2,1,0:T(8,128)(2,1)S(1)} collective-permute-done((bf16[2,192,512]{2,1,0:T(8,128)(2,1)S(1)}, bf16[2,192,512]{2,1,0:T(8,128)(2,1)S(1)}, u32[]{:S(2)}, u32[]{:S(2)}) %collective-permute-start.1) | collective-permute-done | bytes 393248 | tf_op jit(solution)/shard_map/ppermute | solution.py:27
  148.4 5.3 %all_to_all.46 = bf16[2,2,192,512]{3,2,1,0:T(8,128)(2,1)S(1)} all-to-all(bf16[2,2,192,512]{3,2,1,0:T(8,128)(2,1)S(1)} %broadcast_in_dim.16), channel_id=1, replica_groups=mesh['y'=4,'z1'=4,'z0'=2,'x'=4,'h'=2,'c'=2] {'c'}, dimensions={0} | all-to-all | bytes 1572864 | tf_op jit(solution)/shard_map/all_to_all | solution.py:13
  155.1 6.2 %all-to-all-start.5 = ((bf16[8,2,48,1024]{3,2,1,0:T(8,128)(2,1)}), bf16[8,2,48,1024]{3,2,1,0:T(8,128)(2,1)S(1)}, u32[]{:S(2)}, u32[]{:S(2)}) async-start(bf16[8,2,48,1024]{3,2,1,0:T(8,128)(2,1)} %broadcast_in_dim.17), calls=%async_computation.5 | async-start | bytes 3145728 | tf_op jit(solution)/shard_map/all_to_all | solution.py:13
  161.3 20.5 %all-to-all-done.5 = bf16[8,2,48,1024]{3,2,1,0:T(8,128)(2,1)S(1)} async-done(((bf16[8,2,48,1024]{3,2,1,0:T(8,128)(2,1)}), bf16[8,2,48,1024]{3,2,1,0:T(8,128)(2,1)S(1)}, u32[]{:S(2)}, u32[]{:S(2)}) %all-to-all-start.5) | async-done | bytes 1572896 | tf_op jit(solution)/shard_map/all_to_all | solution.py:13
  182.8 43.4 %all_to_all.47 = bf16[16,32,1024]{2,1,0:T(8,128)(2,1)S(1)} all-to-all(bf16[16,32,1024]{2,1,0:T(8,128)(2,1)S(1)} %bitcast.72), channel_id=1, replica_groups=mesh['y'=4,'z1'=4,'z0'=2,'x'=4,'h'=2,'c'=2] {'y','z1'}, dimensions={0} | all-to-all | bytes 2097152 | tf_op jit(solution)/shard_map/all_to_all | solution.py:13
  227.2 32.1 %all_to_all.48 = bf16[16,32,1024]{2,1,0:T(8,128)(2,1)S(1)} all-to-all(bf16[16,32,1024]{2,1,0:T(8,128)(2,1)S(1)} %broadcast_in_dim.18), channel_id=1, replica_groups=mesh['y'=4,'z1'=4,'z0'=2,'x'=4,'h'=2,'c'=2] {'y','z1'}, dimensions={0} | all-to-all | bytes 2097152 | tf_op jit(solution)/shard_map/all_to_all | solution.py:13
  260.1 21.1 %all_to_all.49 = f32[32,1,192]{2,1,0:T(1,128)S(1)} all-to-all(f32[32,1,192]{2,1,0:T(1,128)S(1)} %reshape.94), channel_id=1, replica_groups=mesh['y'=4,'z1'=4,'z0'=2,'x'=4,'h'=2,'c'=2] {'z0','x','h','c'}, dimensions={0} | all-to-all | bytes 49152 | tf_op jit(solution)/shard_map/all_to_all | solution.py:13
  (50 shorter events, 14.1 us)
Async XLA Ops:
  3.1 14.2 %copy-start.1 = (bf16[48,4096]{1,0:T(8,128)(2,1)S(1)}, bf16[48,4096]{1,0:T(8,128)(2,1)}, u32[]{:S(2)}) copy-start(bf16[48,4096]{1,0:T(8,128)(2,1)} %param.8) | copy-start | bytes 1179652
  3.1 66.2 %all-to-all-start = ((bf16[16,64,1024]{2,1,0:T(8,128)(2,1)}), bf16[16,64,1024]{2,1,0:T(8,128)(2,1)S(1)}, u32[]{:S(2)}, u32[]{:S(2)}) async-start(bf16[16,64,1024]{2,1,0:T(8,128)(2,1)} %broadcast_in_dim.14), calls=%async_computation | async-start | bytes 4194304 | tf_op jit(solution)/shard_map/all_to_all | solution.py:13
  17.3 2.5 copy-start.2
  30.3 5.6 %copy-start.4 = (bf16[48,1024]{1,0:T(8,128)(2,1)S(1)}, bf16[48,1024]{1,0:T(8,128)(2,1)}, u32[]{:S(2)}) copy-start(bf16[48,1024]{1,0:T(8,128)(2,1)} %param.12) | copy-start | bytes 294916
  30.3 5.6 %copy-start.5 = (bf16[48,1024]{1,0:T(8,128)(2,1)S(1)}, bf16[48,1024]{1,0:T(8,128)(2,1)}, u32[]{:S(2)}) copy-start(bf16[48,1024]{1,0:T(8,128)(2,1)} %param.7) | copy-start | bytes 294916
  31.2 31.6 %collective-permute-start = (bf16[2,48,1024]{2,1,0:T(8,128)(2,1)S(1)}, bf16[2,48,1024]{2,1,0:T(8,128)(2,1)S(1)}, u32[]{:S(2)}, u32[]{:S(2)}) collective-permute-start(bf16[2,48,1024]{2,1,0:T(8,128)(2,1)S(1)} %get-tuple-element.21), channel_id=1, source_target_pairs={{0,2},{2,0},{1,3},{3,1},{4,6},{6,4},{5,7},{7,5},{8,10},{10,8},{9,1... | collective-permute-start | bytes 589832 | tf_op jit(solution)/shard_map/ppermute | solution.py:27
  70.7 45.6 %all-to-all-start.1 = ((bf16[8,2,48,1024]{3,2,1,0:T(8,128)(2,1)}), bf16[8,2,48,1024]{3,2,1,0:T(8,128)(2,1)}, u32[]{:S(2)}, u32[]{:S(2)}) async-start(bf16[8,2,48,1024]{3,2,1,0:T(8,128)(2,1)} %broadcast_in_dim.15), calls=%async_computation.1 | async-start | bytes 3145728 | tf_op jit(solution)/shard_map/all_to_all | solution.py:13
  78.5 36.2 %collective-permute-start.3 = (bf16[512,1024]{1,0:T(8,128)(2,1)S(1)}, bf16[512,1024]{1,0:T(8,128)(2,1)S(1)}, u32[]{:S(2)}, u32[]{:S(2)}) collective-permute-start(bf16[512,1024]{1,0:T(8,128)(2,1)S(1)} %bitcast.70), channel_id=1, source_target_pairs={{0,16},{16,32},{32,48},{48,64},{64,80},{80,96},{96,112},{112,0},{1... | collective-permute-start | bytes 3145736 | tf_op jit(solution)/shard_map/ppermute | solution.py:23
  81.9 6.3 %collective-permute-start.2 = (bf16[2,2,48,1024]{3,2,1,0:T(8,128)(2,1)S(1)}, bf16[2,2,48,1024]{3,2,1,0:T(8,128)(2,1)S(1)}, u32[]{:S(2)}, u32[]{:S(2)}) collective-permute-start(bf16[2,2,48,1024]{3,2,1,0:T(8,128)(2,1)S(1)} %maximum_select_fusion.1), channel_id=1, source_target_pairs={{0,1},{1,0},{2,3},{3,2},{4,5},{5,4},{6,7},{7,6},{8,9},{9,8},{10,11... | collective-permute-start | bytes 1179656 | tf_op jit(solution)/shard_map/ppermute | solution.py:27
  116.3 1.7 copy-start
  126.1 16.0 %all-to-all-start.4 = ((bf16[4,2,48,1024]{3,2,1,0:T(8,128)(2,1)}), bf16[4,2,48,1024]{3,2,1,0:T(8,128)(2,1)S(1)}, u32[]{:S(2)}, u32[]{:S(2)}) async-start(bf16[4,2,48,1024]{3,2,1,0:T(8,128)(2,1)} %bitcast.67), calls=%async_computation.4 | async-start | bytes 1572864 | tf_op jit(solution)/shard_map/all_to_all | solution.py:13
  130.5 17.8 %collective-permute-start.1 = (bf16[2,192,512]{2,1,0:T(8,128)(2,1)S(1)}, bf16[2,192,512]{2,1,0:T(8,128)(2,1)S(1)}, u32[]{:S(2)}, u32[]{:S(2)}) collective-permute-start(bf16[2,192,512]{2,1,0:T(8,128)(2,1)S(1)} %reduce_sum.51), channel_id=1, source_target_pairs={{0,2},{2,0},{1,3},{3,1},{4,6},{6,4},{5,7},{7,5},{8,10},{10,8},{9,1... | collective-permute-start | bytes 1179656 | tf_op jit(solution)/shard_map/ppermute | solution.py:27
  155.1 26.7 %all-to-all-start.5 = ((bf16[8,2,48,1024]{3,2,1,0:T(8,128)(2,1)}), bf16[8,2,48,1024]{3,2,1,0:T(8,128)(2,1)S(1)}, u32[]{:S(2)}, u32[]{:S(2)}) async-start(bf16[8,2,48,1024]{3,2,1,0:T(8,128)(2,1)} %broadcast_in_dim.17), calls=%async_computation.5 | async-start | bytes 3145728 | tf_op jit(solution)/shard_map/all_to_all | solution.py:13
  182.7 43.6 %copy-start.3 = (f32[32,1024]{1,0:T(8,128)S(1)}, f32[32,1024]{1,0:T(8,128)}, u32[]{:S(2)}) copy-start(f32[32,1024]{1,0:T(8,128)} %param.11) | copy-start | bytes 393220
